TPU v7x, 32 devices: a whole 2x2x4 slice. The times are simulated.
32 devices in a mesh: gx: 8 (over z, x), gy: 4 (over y, core).
Axes of the slice: x: 2, y: 2, z: 4, core: 2. Of those that a mesh axis runs over, the one named last changes fastest.
Arguments:
- velocity: float32 [3, 1, 1024, 2560], P(None, None, 'gy', 'gx'), may hold values from -12 to 12
- grid_x: float32 [33], replicated, may hold values from 0.05 to 1
- grid_y: float32 [1024, 33], P('gy'), may hold values from 0.05 to 1
- test_x: float32 [33], replicated, may hold values from 0.05 to 1
- test_y: float32 [1024, 33], P('gy'), may hold values from 0.05 to 1
Outputs:
- subgrid: float32 [6, 1, 1024, 2560], P(None, None, 'gy', 'gx')
- germano: float32 [6, 1, 1024, 2560], P(None, None, 'gy', 'gx')
All inputs are finite; a program needn't handle non-finite values.
Results may differ from a plain program's by a relative error of at most 0.0001.
Values sent between devices are 32-bit elements; how exact they have to be, the bound alone decides.
A program may use at most 64 MiB of HBM per device.

v0:
```python
import functools

import jax
import jax.numpy as jnp
from jax import lax
from jax.experimental import pallas as pl
from jax.experimental.pallas import tpu as pltpu
from jax.sharding import PartitionSpec as P

MESH = pl.DeviceIdType.MESH
LANES = 128
SUB = 8
DIRECTIONS = [(1, 0), (-1, 0), (0, 1), (0, -1), (1, 1), (-1, 1), (1, -1), (-1, -1)]
BF = jnp.bfloat16
F32 = jnp.float32


def round_up(value, unit):
    return (value + unit - 1) // unit * unit


def split(value):
    high = value.astype(BF)
    return high, (value - high.astype(F32)).astype(BF)


def pair_of(p):
    first = jnp.where(p < 3, 0, jnp.where(p < 5, 1, 2))
    second = jnp.where(p < 3, p, jnp.where(p < 5, p - 2, 2))
    return first, second


def dot(a, b):
    return jnp.dot(a, b, preferred_element_type=F32)


def x_weights(w_ref, step, out):
    taps = w_ref.shape[1]
    w = jnp.concatenate([w_ref[...], jnp.zeros((1, LANES - taps), F32)], axis=1)
    w = w / jnp.sum(w)
    band = pltpu.roll(jnp.broadcast_to(w, (LANES, LANES)), 0, 1, stride=1, stride_axis=0)
    high, low = split(band[0:step])
    out[0:step, 0:LANES] = high
    out[0:step, LANES:] = high
    out[step:, 0:LANES] = low
    out[step:, LANES:] = jnp.zeros((step, LANES), BF)


def y_weights(table, taps, first_row, total, cols, main, edge=None, tiles=None):
    margin = (taps - 1) // 2
    lanes = table.shape[1]
    wide = cols + LANES
    k = lax.broadcasted_iota(jnp.int32, (LANES, lanes), 0)
    lane = lax.broadcasted_iota(jnp.int32, (LANES, lanes), 1)
    y = first_row + jnp.where(lane < cols + LANES // 2, lane, lane - wide)
    source = y + k - margin
    keep = (k < taps) & (source >= 0) & (source < total) & (y >= 0) & (y < total)
    w = jnp.where(keep, jnp.concatenate(
        [table, jnp.zeros((LANES - table.shape[0], lanes), F32)], axis=0), 0.0)
    s = jnp.sum(w, axis=0, keepdims=True)
    w = (w / jnp.where(s > 0.0, s, 1.0)).T
    zeros = jnp.zeros((LANES, cols), F32)
    for t in (range(lanes // LANES) if tiles is None else tiles):
        at = slice(t * LANES, (t + 1) * LANES)
        tile = jnp.concatenate([w[at], zeros], axis=1)
        band = pltpu.roll(tile, (t * LANES - margin) % wide, 1, stride=1, stride_axis=0)
        if t * LANES < cols:
            own, halo = band[:, 0:cols].T, band[:, cols:]
            own_high, own_low = split(own)
            main[0:cols, at] = own_high
            main[cols:2 * cols, at] = own_low
            main[2 * cols:3 * cols, at] = own_high
            high = halo.astype(BF).astype(F32)
            packed = high + pltpu.roll(high, 2 * margin, 1) + pltpu.roll(halo - high, 4 * margin, 1)
            main[3 * cols:, at] = packed.T.astype(BF)
        else:
            edge_high, edge_low = split(band.T)
            at = 0
            for lo, hi in ((0, cols), (cols, wide)):
                for part in (edge_high, edge_low, edge_high):
                    edge[at:at + hi - lo] = part[lo:hi]
                    at += hi - lo


def halo_kernel(nx, ny, width, v_hbm, t_hbm, gx_hbm, tx_hbm, ty_hbm,
                ext_ref, gxw, txw, gym, gye, tym,
                v_ref, t_ref, gx_ref, tx_ref, ty_ref, text_ref, load_sem, pack_d, pack_u, from_d, from_u, from_l, from_r, corners, t_low, t_high,
                send_sem, recv_sem):
    comps, rows, cols = v_ref.shape
    taps = t_ref.shape[0]
    margin = width // 2
    me_x, me_y = lax.axis_index("gx"), lax.axis_index("gy")

    def device(dx, dy):
        return {"gx": lax.rem(me_x + dx + nx, nx), "gy": lax.rem(me_y + dy + ny, ny)}

    barrier = pltpu.get_barrier_semaphore()
    for dx, dy in DIRECTIONS:
        pl.semaphore_signal(barrier, inc=1, device_id=device(dx, dy), device_id_type=MESH)

    loads = [pltpu.make_async_copy(src, dst, load_sem.at[i]) for i, (src, dst) in enumerate((
        (v_hbm, v_ref), (t_hbm, t_ref), (gx_hbm, gx_ref), (tx_hbm, tx_ref), (ty_hbm, ty_ref)))]
    for load in loads:
        load.start()
    per = LANES // width
    groups = rows // width
    loads[0].wait()
    for c in range(comps):
        for g in range(groups):
            for q in range(per):
                src = pl.ds(g * width + q * SUB, SUB)
                dst = pl.ds(g * SUB, SUB)
                pack_u[c, dst, q * width:(q + 1) * width] = v_ref[c, src, cols - width:cols]
                pack_d[c, dst, q * width:(q + 1) * width] = v_ref[c, src, 0:width]
    pl.semaphore_wait(barrier, len(DIRECTIONS))

    loads[1].wait()
    first, last = pl.ds(0, SUB), pl.ds((groups - 1) * SUB, SUB)
    sources = [
        v_hbm.at[:, pl.ds(rows - width, width), :], v_hbm.at[:, pl.ds(0, width), :],
        pack_u, pack_d,
        pack_u.at[:, last, :], pack_u.at[:, first, :], pack_d.at[:, last, :], pack_d.at[:, first, :],
    ]
    targets = [from_l, from_r, from_d, from_u] + [corners.at[i] for i in range(4)]
    copies = []
    for i, (dx, dy) in enumerate(DIRECTIONS):
        copies.append((dy, pltpu.make_async_remote_copy(
            src_ref=sources[i], dst_ref=targets[i], send_sem=send_sem.at[i],
            recv_sem=recv_sem.at[i], device_id=device(dx, dy), device_id_type=MESH)))
    for i, (dy, src, dst) in enumerate([
        (1, t_ref.at[:, pl.ds(cols - LANES, LANES)], t_low),
        (-1, t_ref.at[:, pl.ds(0, LANES)], t_high),
    ]):
        n = len(DIRECTIONS) + i
        copies.append((dy, pltpu.make_async_remote_copy(
            src_ref=src, dst_ref=dst, send_sem=send_sem.at[n],
            recv_sem=recv_sem.at[n], device_id=device(0, dy), device_id_type=MESH)))

    has_up, has_down = me_y < ny - 1, me_y > 0
    for dy, copy in copies:
        if dy == 0:
            copy.start()
    for sign, present in ((1, has_up), (-1, has_down)):
        @pl.when(present)
        def _(sign=sign):
            for dy, copy in copies:
                if dy == sign:
                    copy.start()

    rows_ext = rows + 2 * width
    ext_ref[:, :, cols:] = jnp.zeros((comps, rows_ext, LANES), F32)
    text_ref[...] = jnp.zeros_like(text_ref)
    for c in range(comps):
        ext_ref[c, pl.ds(width, rows), 0:cols] = v_ref[c]
    text_ref[0:taps, 0:cols] = t_ref[...]
    for load in loads[2:]:
        load.wait()
    first_row, total = me_y * cols, cols * ny
    x_weights(gx_ref, gxw.shape[0] // 2, gxw)
    x_weights(tx_ref, txw.shape[0] // 2, txw)
    own_tiles = range(cols // LANES)
    y_weights(t_ref[...], taps, first_row, total, cols, gym, tiles=own_tiles)
    y_weights(ty_ref[...], taps, first_row, total, cols, tym, tiles=own_tiles)

    def unpack(buf, c, row, lane, count):
        for g in range(count):
            for q in range(per):
                ext_ref[c, pl.ds(row + g * width + q * SUB, SUB), lane:lane + width] = (
                    buf[c, pl.ds(g * SUB, SUB), q * width:(q + 1) * width])

    for sign, present, lane, mid, pair, tile, at in (
        (1, has_down, cols + LANES - width, from_d, (0, 1), t_low, LANES - margin),
        (-1, has_up, cols, from_u, (2, 3), t_high, 0),
    ):
        @pl.when(present)
        def _(sign=sign, lane=lane, mid=mid, pair=pair, tile=tile, at=at):
            for dy, copy in copies:
                if dy == sign:
                    copy.wait_recv()
            for c in range(comps):
                unpack(mid, c, width, lane, groups)
                unpack(corners.at[pair[0]], c, 0, lane, 1)
                unpack(corners.at[pair[1]], c, width + rows, lane, 1)
            text_ref[0:taps, cols + at:cols + at + margin] = tile[:, at:at + margin]

    y_weights(text_ref[...], taps, first_row, total, cols, gym, gye, tiles=(cols // LANES,))
    copies[0][1].wait_recv()
    for c in range(comps):
        ext_ref[c, pl.ds(0, width), 0:cols] = from_l[c]
    copies[1][1].wait_recv()
    for c in range(comps):
        ext_ref[c, pl.ds(width + rows, width), 0:cols] = from_r[c]

    for dy, copy in copies:
        if dy == 0:
            copy.wait_send()
    for sign, present in ((1, has_up), (-1, has_down)):
        @pl.when(present)
        def _(sign=sign):
            for dy, copy in copies:
                if dy == sign:
                    copy.wait_send()


def y_filter(value, margin, cols, main, put, edge=None):
    high, low = split(value[:, 0:cols])
    halo = value[:, cols:]
    lane = lax.broadcasted_iota(jnp.int32, halo.shape, 1)
    near = jnp.where((lane < margin) | (lane >= LANES - margin), halo, 0.0)
    near_high = near.astype(BF).astype(F32)
    packed = near_high + pltpu.roll(near - near_high, 2 * margin, 1) + pltpu.roll(near_high, 4 * margin, 1)
    put(dot(jnp.concatenate([high, high, low, packed.astype(BF)], axis=1), main[...]), slice(0, cols))
    if edge is not None:
        hh, hl = split(halo)
        put(dot(jnp.concatenate([high, high, low, hh, hh, hl], axis=1), edge[...]),
            slice(cols, cols + LANES))


def x_filter(zh, zl, start, count, lanes, weights, put):
    step = weights.shape[0] // 2
    for s in range(0, count, step):
        size = min(step, count - s)
        at = slice(start + s, start + s + LANES)
        data = jnp.concatenate([zh[at, lanes], zl[at, lanes]], axis=0)
        if size == step:
            r = dot(weights[...], data)
        else:
            r = dot(jnp.concatenate([weights[0:size], weights[step:step + size]], axis=0), data)
        put(s, size, r[0:size] + r[size:])


def stress_kernel(margin, batch, ext_ref, gxw, txw, gym, gye, tym, sub_ref, ger_ref,
                  coarse, tested, sub, ger, zh, zl, sems):
    comps, rows_ext, wide = ext_ref.shape
    pairs, rows, cols = sub_ref.shape
    rows_mid = rows + 2 * margin
    own = slice(0, cols)
    everything = slice(0, wide)
    for slot in range(zh.shape[0]):
        zh[slot, pl.ds(rows_ext, LANES), :] = jnp.zeros((LANES, wide), BF)
        zl[slot, pl.ds(rows_ext, LANES), :] = jnp.zeros((LANES, wide), BF)

    def store(slot, n, count):
        def put(z, lanes):
            high, low = split(z)
            for b in range(n):
                at = slice(b * count, (b + 1) * count)
                zh[slot + b, 0:count, lanes], zl[slot + b, 0:count, lanes] = high[at], low[at]
        return put

    def stacked(values):
        return jnp.concatenate(values, axis=0)

    y_filter(stacked([ext_ref[c] for c in range(comps)]), margin, cols, gym,
             store(0, comps, rows_ext), gye)
    for c in range(comps):
        def put(start, size, value, c=c):
            coarse[c, pl.ds(start, size), :] = value

        x_filter(zh.at[c], zl.at[c], 0, rows_mid, everything, gxw, put)
    y_filter(stacked([coarse[c] for c in range(comps)]), margin, cols, tym,
             store(0, comps, rows_mid))
    for c in range(comps):
        def put_tested(start, size, value, c=c):
            tested[c, pl.ds(start, size), :] = value

        x_filter(zh.at[c], zl.at[c], 0, rows, own, txw, put_tested)

    def leave(which, source, target, p):
        return pltpu.make_async_copy(source.at[p], target.at[p], sems.at[which, p])

    mid = pl.ds(margin, rows_mid)

    @pl.loop(0, pairs // batch)
    def _(step):
        indices = [(step * batch + b,) + pair_of(step * batch + b) for b in range(batch)]
        y_filter(stacked([ext_ref[i, mid, :] * ext_ref[j, mid, :] for _, i, j in indices]),
                 margin, cols, gym, store(0, batch, rows_mid))
        y_filter(stacked([coarse[i] * coarse[j] for _, i, j in indices]),
                 margin, cols, tym, store(batch, batch, rows_mid))
        for b, (p, i, j) in enumerate(indices):
            def put_sub(start, size, value, p=p, i=i, j=j):
                at = pl.ds(margin + start, size)
                sub[p, pl.ds(start, size), :] = value - coarse[i, at, own] * coarse[j, at, own]

            x_filter(zh.at[b], zl.at[b], 0, rows, own, gxw, put_sub)
        for b, (p, i, j) in enumerate(indices):
            def put_ger(start, size, value, p=p, i=i, j=j):
                at = pl.ds(start, size)
                ger[p, at, :] = value - tested[i, at, :] * tested[j, at, :]

            x_filter(zh.at[batch + b], zl.at[batch + b], 0, rows, own, txw, put_ger)
        for p, _, _ in indices:
            leave(0, sub, sub_ref, p).start()
            leave(1, ger, ger_ref, p).start()

    @pl.loop(0, pairs)
    def _(p):
        leave(0, sub, sub_ref, p).wait()
        leave(1, ger, ger_ref, p).wait()


def local(nx, ny, velocity, grid_x, grid_y, test_x, test_y):
    comps, planes, cols, rows = velocity.shape
    taps = grid_x.shape[0]
    margin = (taps - 1) // 2
    width = 2 * margin
    wide = cols + LANES
    step = LANES - width
    pairs = comps * (comps + 1) // 2
    batch = 2
    slots = max(comps, 2 * batch)
    vmem = pl.BlockSpec(memory_space=pltpu.VMEM)
    anywhere = pl.BlockSpec(memory_space=pl.ANY)
    packed = rows // width * SUB
    subs, gers = [], []
    rows_mid, rows_ext = rows + width, rows + 2 * width
    for plane in range(planes):
        v = jnp.swapaxes(velocity[:, plane], 1, 2)
        ext, *weights = pl.pallas_call(
            functools.partial(halo_kernel, nx, ny, width),
            out_shape=(
                jax.ShapeDtypeStruct((comps, rows_ext, wide), F32),
                jax.ShapeDtypeStruct((2 * step, 2 * LANES), BF),
                jax.ShapeDtypeStruct((2 * step, 2 * LANES), BF),
                jax.ShapeDtypeStruct((3 * cols + LANES, cols), BF),
                jax.ShapeDtypeStruct((3 * wide, LANES), BF),
                jax.ShapeDtypeStruct((3 * cols + LANES, cols), BF),
            ),
            in_specs=[pl.BlockSpec(memory_space=pltpu.HBM)] * 5,
            out_specs=(vmem,) * 6,
            scratch_shapes=[
                pltpu.VMEM((comps, rows, cols), F32),
                pltpu.VMEM((taps, cols), F32),
                pltpu.VMEM((1, taps), F32),
                pltpu.VMEM((1, taps), F32),
                pltpu.VMEM((taps, cols), F32),
                pltpu.VMEM((round_up(taps, SUB), wide), F32),
                pltpu.SemaphoreType.DMA((5,)),
                pltpu.VMEM((comps, packed, LANES), F32),
                pltpu.VMEM((comps, packed, LANES), F32),
                pltpu.VMEM((comps, packed, LANES), F32),
                pltpu.VMEM((comps, packed, LANES), F32),
                pltpu.VMEM((comps, width, cols), F32),
                pltpu.VMEM((comps, width, cols), F32),
                pltpu.VMEM((4, comps, SUB, LANES), F32),
                pltpu.VMEM((taps, LANES), F32),
                pltpu.VMEM((taps, LANES), F32),
                pltpu.SemaphoreType.DMA((len(DIRECTIONS) + 2,)),
                pltpu.SemaphoreType.DMA((len(DIRECTIONS) + 2,)),
            ],
            compiler_params=pltpu.CompilerParams(
                collective_id=plane, has_side_effects=True, vmem_limit_bytes=48 << 20),
            name="halo",
        )(*[pltpu.with_memory_space_constraint(x, pltpu.HBM) for x in (
            v, grid_y.T, grid_x.reshape(1, taps), test_x.reshape(1, taps), test_y.T)])
        out = jax.ShapeDtypeStruct((pairs, rows, cols), F32)
        sub, ger = pl.pallas_call(
            functools.partial(stress_kernel, margin, batch),
            out_shape=(out, out),
            in_specs=[vmem] * 6,
            out_specs=(anywhere, anywhere),
            scratch_shapes=[
                pltpu.VMEM((comps, rows_mid, wide), F32),
                pltpu.VMEM((comps, rows, cols), F32),
                pltpu.VMEM((pairs, rows, cols), F32),
                pltpu.VMEM((pairs, rows, cols), F32),
                pltpu.VMEM((slots, rows_ext + LANES, wide), BF),
                pltpu.VMEM((slots, rows_ext + LANES, wide), BF),
                pltpu.SemaphoreType.DMA((2, pairs)),
            ],
            compiler_params=pltpu.CompilerParams(vmem_limit_bytes=48 << 20),
            name="stress",
        )(ext, *weights)
        subs.append(jnp.swapaxes(sub, 1, 2))
        gers.append(jnp.swapaxes(ger, 1, 2))
    return jnp.stack(subs, axis=1), jnp.stack(gers, axis=1)


def solution(mesh):
    nx, ny = mesh.shape["gx"], mesh.shape["gy"]
    field = P(None, None, "gy", "gx")
    return jax.shard_map(
        functools.partial(local, nx, ny),
        mesh=mesh,
        in_specs=(field, P(), P("gy", None), P(), P("gy", None)),
        out_specs=(field, field),
        check_vma=False,
    )
```

profile of v0, /device:TPU:0, one launch (start us, length us, event | category | flops | bytes accessed | tf_op | source)
XLA Modules:
  0.0 21.9 jit_solution(3440858399326031281)
XLA Ops:
  0.6 12.5 %halo.1 = (f32[3,384,384]{2,1,0:T(8,128)S(1)}, bf16[192,256]{1,0:T(8,128)(2,1)S(1)}, bf16[192,256]{1,0:T(8,128)(2,1)S(1)}, bf16[896,256]{1,0:T(8,128)(2,1)S(1)},...) custom-call(f32[3,320,256]{2,1,0:T(8,128)} %bitcast.17, f32[33,256]{1,0:T(8,128)} %bitcast.18, ...), custom_call_target="tpu_custom_call" | custom-call | tf_op jit(solution)/shard_map/halo/pallas_call | solution.py:320
  13.1 8.7 %stress.1 = (f32[6,320,256]{2,1,0:T(8,128)}, f32[6,320,256]{2,1,0:T(8,128)}) custom-call(f32[3,384,384]{2,1,0:T(8,128)S(1)} %get-tuple-element.10.ext_ref, bf16[192,256]{1,0:T(8,128)(2,1)S(1)} %get-tuple-element.11.gxw, bf16[192,256]{1,0:T(8,128)(2,1)S(1)} %get-tuple-element.12.txw, bf16[896,256]{1,0:T(8,128)(2,1)S(1)} %get-tuple-element.13.gym, ...), custom_call_target="tpu_custom_call" | custom-call | tf_op jit(solution)/shard_map/stress/pallas_call | solution.py:358
where the time goes:
time: 22 us; the launch traced here: 21.9 us
  Pallas kernels  21.2 us (96%)
  between operations  0.64 us (3%)
    pallas_call x1, Pallas kernels, local(): pl.pallas_call(functools.partial(halo_kernel, nx, ny, width), out_shape=(...  12.5 us
    pallas_call x1, Pallas kernels, local(): pl.pallas_call(functools.partial(stress_kernel, margin, batch), out_shape...  8.74 us

commit v1 on v0

v1 whole, which is shorter than its diff:
```python
import functools

import jax
import jax.numpy as jnp
from jax import lax
from jax.experimental import pallas as pl
from jax.experimental.pallas import tpu as pltpu
from jax.sharding import PartitionSpec as P

MESH = pl.DeviceIdType.MESH
LANES = 128
SUB = 8
DIRECTIONS = [(1, 0), (-1, 0), (0, 1), (0, -1), (1, 1), (-1, 1), (1, -1), (-1, -1)]
BF = jnp.bfloat16
F32 = jnp.float32


def round_up(value, unit):
    return (value + unit - 1) // unit * unit


def split(value):
    high = value.astype(BF)
    return high, (value - high.astype(F32)).astype(BF)


def pair_of(p):
    first = jnp.where(p < 3, 0, jnp.where(p < 5, 1, 2))
    second = jnp.where(p < 3, p, jnp.where(p < 5, p - 2, 2))
    return first, second


def dot(a, b):
    return jnp.dot(a, b, preferred_element_type=F32)


def x_weights(w_ref, step, out, edge):
    taps = w_ref.shape[1]
    w = jnp.concatenate([w_ref[...], jnp.zeros((1, LANES - taps), F32)], axis=1)
    w = w / jnp.sum(w)
    band = pltpu.roll(jnp.broadcast_to(w, (LANES, LANES)), 0, 1, stride=1, stride_axis=0)
    high, low = split(band[0:step])
    out[0:step, 0:LANES] = high
    out[0:step, LANES:] = high
    out[step:, 0:LANES] = low
    out[step:, LANES:] = jnp.zeros((step, LANES), BF)
    width = edge.shape[0]
    high, low = split(band[0:width])
    high = high.astype(F32)
    edge[:, 0:LANES] = (high + pltpu.roll(high, 2 * width, 1)).astype(BF)
    edge[:, LANES:] = low


def y_weights(table, taps, first_row, total, cols, main, edge=None, tiles=None):
    margin = (taps - 1) // 2
    width = 2 * margin
    lanes = table.shape[1]
    wide = cols + LANES
    k = lax.broadcasted_iota(jnp.int32, (LANES, lanes), 0)
    lane = lax.broadcasted_iota(jnp.int32, (LANES, lanes), 1)
    y = first_row + jnp.where(lane < cols + LANES // 2, lane, lane - wide)
    source = y + k - margin
    keep = (k < taps) & (source >= 0) & (source < total) & (y >= 0) & (y < total)
    w = jnp.where(keep, jnp.concatenate(
        [table, jnp.zeros((LANES - table.shape[0], lanes), F32)], axis=0), 0.0)
    s = jnp.sum(w, axis=0, keepdims=True)
    w = (w / jnp.where(s > 0.0, s, 1.0)).T
    zeros = jnp.zeros((LANES, cols), F32)
    for t in (range(lanes // LANES) if tiles is None else tiles):
        at = slice(t * LANES, (t + 1) * LANES)
        tile = jnp.concatenate([w[at], zeros], axis=1)
        band = pltpu.roll(tile, (t * LANES - margin) % wide, 1, stride=1, stride_axis=0)
        if t * LANES < cols:
            own, halo = band[:, 0:cols].T, band[:, cols:]
            own_high, own_low = split(own)
            main[0:cols, at] = own_high
            main[cols:2 * cols, at] = own_low
            main[2 * cols:3 * cols, at] = own_high
            high = halo.astype(BF).astype(F32)
            packed = high + pltpu.roll(high, 2 * margin, 1) + pltpu.roll(halo - high, 4 * margin, 1)
            main[3 * cols:, at] = packed.T.astype(BF)
        else:
            low_own, high_own, halo = band[:, 0:LANES].T, band[:, cols - LANES:cols].T, band[:, cols:].T
            near = jnp.concatenate([
                halo[0:width], low_own[0:LANES // 2 - width], high_own[LANES // 2 + width:],
                halo[LANES - width:]], axis=0)
            high, low = split(near)
            edge[0:LANES] = high
            edge[LANES:2 * LANES] = high
            edge[2 * LANES:] = low


def y_filter(value, margin, cols, main, put, edge=None):
    high, low = split(value[:, 0:cols])
    halo = value[:, cols:]
    lane = lax.broadcasted_iota(jnp.int32, halo.shape, 1)
    near = jnp.where((lane < margin) | (lane >= LANES - margin), halo, 0.0)
    near_high = near.astype(BF).astype(F32)
    packed = near_high + pltpu.roll(near - near_high, 2 * margin, 1) + pltpu.roll(near_high, 4 * margin, 1)
    put(dot(jnp.concatenate([high, high, low, packed.astype(BF)], axis=1), main[...]), slice(0, cols))
    if edge is not None:
        width = 2 * margin
        own = jnp.where(lane < LANES // 2, pltpu.roll(value[:, 0:LANES], width, 1),
                        pltpu.roll(value[:, cols - LANES:cols], LANES - width, 1))
        ends = jnp.where((lane < width) | (lane >= LANES - width), halo, own)
        high, low = split(ends)
        put(dot(jnp.concatenate([high, low, high], axis=1), edge[...]), slice(cols, cols + LANES))


def x_filter(zh, zl, start, count, lanes, weights, put):
    step = weights.shape[0] // 2
    for s in range(0, count, step):
        size = min(step, count - s)
        at = slice(start + s, start + s + LANES)
        data = jnp.concatenate([zh[at, lanes], zl[at, lanes]], axis=0)
        if size == step:
            r = dot(weights[...], data)
        else:
            r = dot(jnp.concatenate([weights[0:size], weights[step:step + size]], axis=0), data)
        put(s, size, r[0:size] + r[size:])


def stacked(values):
    return jnp.concatenate(values, axis=0)


def interior_kernel(nx, ny, width, batch, v_hbm, t_hbm, gx_hbm, tx_hbm, ty_hbm,
                    halo, corners, z1h, z1l, zph, zpl, z2h, z2l, sub, ger, gxe, txe, gym, gye, tym,
                    ext, v_ref, t_ref, gx_ref, tx_ref, ty_ref, text_ref, gxw, txw,
                    pack_d, pack_u, from_d, from_u, t_low, t_high,
                    coarse, tested, zh, zl, load_sem, send_sem, recv_sem, ready):
    comps, rows, cols = v_ref.shape
    taps = t_ref.shape[0]
    margin = width // 2
    pairs, inner, _ = sub.shape
    innermost = ger.shape[1]
    me_x, me_y = lax.axis_index("gx"), lax.axis_index("gy")
    first, last = me_x == 0, me_x == nx - 1
    has_up, has_down = me_y < ny - 1, me_y > 0
    vertical = jnp.where(has_up, 1, 0) + jnp.where(has_down, 1, 0)
    not_first, not_last = me_x > 0, me_x < nx - 1
    sides = ((1, has_up), (-1, has_down))

    def device(dx, dy):
        return {"gx": lax.rem(me_x + dx + nx, nx), "gy": lax.rem(me_y + dy + ny, ny)}

    def signal(sem, dx, dy):
        pl.semaphore_signal(sem, inc=1, device_id=device(dx, dy), device_id_type=MESH)

    barrier = pltpu.get_barrier_semaphore()
    signal(barrier, -1, 0)
    pl.when(not_last)(lambda: signal(barrier, 1, 0))
    for sign, present in sides:
        @pl.when(present)
        def _(sign=sign):
            signal(barrier, 0, sign)
            signal(barrier, -1, sign)

        pl.when(present & not_last)(lambda sign=sign: signal(barrier, 1, sign))

    loads = [pltpu.make_async_copy(src, dst, load_sem.at[i]) for i, (src, dst) in enumerate((
        (v_hbm, v_ref), (t_hbm, t_ref), (gx_hbm, gx_ref), (tx_hbm, tx_ref), (ty_hbm, ty_ref)))]
    for load in loads:
        load.start()
    per = LANES // width
    groups = rows // width
    loads[0].wait()
    for c in range(comps):
        for g in range(groups):
            for q in range(per):
                src = pl.ds(g * width + q * SUB, SUB)
                dst = pl.ds(g * SUB, SUB)
                pack_u[c, dst, q * width:(q + 1) * width] = v_ref[c, src, cols - width:cols]
                pack_d[c, dst, q * width:(q + 1) * width] = v_ref[c, src, 0:width]
    pl.semaphore_wait(barrier, 1 + 2 * vertical + jnp.where(first, 0, 1 + vertical))

    head, tail = pl.ds(0, SUB), pl.ds((groups - 1) * SUB, SUB)
    sources = [
        v_hbm.at[:, pl.ds(rows - width, width), :], v_hbm.at[:, pl.ds(0, width), :],
        pack_u, pack_d,
        pack_u.at[:, tail, :], pack_u.at[:, head, :], pack_d.at[:, tail, :], pack_d.at[:, head, :],
    ]
    targets = [halo.at[0], halo.at[1], from_d, from_u] + [corners.at[i] for i in range(4)]
    copies = {}
    for i, where in enumerate(DIRECTIONS):
        copies[where] = pltpu.make_async_remote_copy(
            src_ref=sources[i], dst_ref=targets[i], send_sem=send_sem.at[i],
            recv_sem=recv_sem.at[i], device_id=device(*where), device_id_type=MESH)
    tables = {}
    for i, (sign, src, dst) in enumerate((
        (1, t_ref.at[:, pl.ds(cols - LANES, LANES)], t_low),
        (-1, t_ref.at[:, pl.ds(0, LANES)], t_high),
    )):
        n = len(DIRECTIONS) + i
        tables[sign] = pltpu.make_async_remote_copy(
            src_ref=src, dst_ref=dst, send_sem=send_sem.at[n],
            recv_sem=recv_sem.at[n], device_id=device(0, sign), device_id_type=MESH)

    copies[1, 0].start()

    @pl.when(last)
    def _():
        signal(ready, 1, 0)
        for sign, present in sides:
            pl.when(present)(lambda sign=sign: signal(ready, 1, sign))

    pl.when(not_first)(lambda: copies[-1, 0].start())
    loads[1].wait()
    for sign, present in sides:
        @pl.when(present)
        def _(sign=sign):
            copies[0, sign].start()
            tables[sign].start()
            copies[1, sign].start()

        pl.when(present & not_first)(lambda sign=sign: copies[-1, sign].start())

    ext[:, :, cols:] = jnp.zeros((comps, rows, LANES), F32)
    text_ref[...] = jnp.zeros_like(text_ref)
    for sign, present in sides:
        @pl.when(jnp.logical_not(present))
        def _(sign=sign):
            for side in range(2):
                corners[side + (2 if sign > 0 else 0)] = jnp.zeros(corners.shape[1:], F32)

    for c in range(comps):
        ext[c, :, 0:cols] = v_ref[c]
    text_ref[0:taps, 0:cols] = t_ref[...]
    for load in loads[2:]:
        load.wait()
    first_row, total = me_y * cols, cols * ny
    x_weights(gx_ref, gxw.shape[0] // 2, gxw, gxe)
    x_weights(tx_ref, txw.shape[0] // 2, txw, txe)
    own_tiles = range(cols // LANES)
    y_weights(t_ref[...], taps, first_row, total, cols, gym, tiles=own_tiles)
    y_weights(ty_ref[...], taps, first_row, total, cols, tym, tiles=own_tiles)
    filled = zh.shape[1]
    for slot in range(zh.shape[0]):
        zh[slot, inner:filled, :] = jnp.zeros((filled - inner, cols + LANES), BF)
        zl[slot, inner:filled, :] = jnp.zeros((filled - inner, cols + LANES), BF)

    for sign, present, lane, mid, tile, at in (
        (1, has_down, cols + LANES - width, from_d, t_low, LANES - margin),
        (-1, has_up, cols, from_u, t_high, 0),
    ):
        @pl.when(present)
        def _(sign=sign, lane=lane, mid=mid, tile=tile, at=at):
            copies[0, sign].wait_recv()
            tables[sign].wait_recv()
            for c in range(comps):
                for g in range(groups):
                    for q in range(per):
                        ext[c, pl.ds(g * width + q * SUB, SUB), lane:lane + width] = (
                            mid[c, pl.ds(g * SUB, SUB), q * width:(q + 1) * width])
            text_ref[0:taps, cols + at:cols + at + margin] = tile[:, at:at + margin]

    y_weights(text_ref[...], taps, first_row, total, cols, gym, gye, tiles=(cols // LANES,))

    own = slice(0, cols)
    everything = slice(0, cols + LANES)

    def store(slot, n, count):
        def put(z, lanes):
            high, low = split(z)
            for b in range(n):
                at = slice(b * count, (b + 1) * count)
                zh[slot + b, 0:count, lanes], zl[slot + b, 0:count, lanes] = high[at], low[at]
        return put

    def keep(slot, count, size, lanes, high, low, index):
        for side, at in enumerate((slice(0, size), slice(count - size, count))):
            high[index, side] = zh[slot, at, lanes]
            low[index, side] = zl[slot, at, lanes]

    y_filter(stacked([ext[c] for c in range(comps)]), margin, cols, gym, store(0, comps, rows), gye)
    for c in range(comps):
        def put(start, size, value, c=c):
            coarse[c, pl.ds(start, size), :] = value

        x_filter(zh.at[c], zl.at[c], 0, inner, everything, gxw, put)
        keep(c, rows, width, everything, z1h, z1l, c)
    y_filter(stacked([coarse[c] for c in range(comps)]), margin, cols, tym, store(0, comps, inner))
    for c in range(comps):
        def put_tested(start, size, value, c=c):
            tested[c, pl.ds(start, size), :] = value

        x_filter(zh.at[c], zl.at[c], 0, innermost, own, txw, put_tested)
        keep(c, inner, width, own, z2h, z2l, c)

    @pl.when(first)
    def _():
        pl.semaphore_wait(ready, 1 + vertical)
        copies[-1, 0].start()
        for sign, present in sides:
            pl.when(present)(lambda sign=sign: copies[-1, sign].start())

    @pl.loop(0, pairs // batch)
    def _(step):
        indices = [(step * batch + b,) + pair_of(step * batch + b) for b in range(batch)]
        y_filter(stacked([ext[i] * ext[j] for _, i, j in indices]), margin, cols, gym, store(0, batch, rows))
        y_filter(stacked([coarse[i] * coarse[j] for _, i, j in indices]),
                 margin, cols, tym, store(batch, batch, inner))
        for b, (p, i, j) in enumerate(indices):
            def put_sub(start, size, value, p=p, i=i, j=j):
                at = pl.ds(start, size)
                sub[p, at, :] = value - coarse[i, at, own] * coarse[j, at, own]

            x_filter(zh.at[b], zl.at[b], 0, inner, own, gxw, put_sub)
            keep(b, rows, width + margin, own, zph, zpl, p)
        for b, (p, i, j) in enumerate(indices):
            def put_ger(start, size, value, p=p, i=i, j=j):
                at = pl.ds(start, size)
                ger[p, at, :] = value - tested[i, at, :] * tested[j, at, :]

            x_filter(zh.at[batch + b], zl.at[batch + b], 0, innermost, own, txw, put_ger)
            keep(batch + b, inner, width, own, z2h, z2l, comps + p)

    copies[1, 0].wait_recv()
    copies[-1, 0].wait_recv()
    for sign, present in ((1, has_down), (-1, has_up)):
        @pl.when(present)
        def _(sign=sign):
            copies[1, sign].wait_recv()
            copies[-1, sign].wait_recv()

    copies[1, 0].wait_send()
    copies[-1, 0].wait_send()
    for sign, present in sides:
        @pl.when(present)
        def _(sign=sign):
            for dx in (0, 1, -1):
                copies[dx, sign].wait_send()
            tables[sign].wait_send()


def edge_kernel(margin, halo, corners, z1h, z1l, zph, zpl, z2h, z2l, sub_in, ger_in,
                gxe, txe, gym, gye, tym, sub_ref, ger_ref, sub_e, ger_e, sems):
    comps, cols = halo.shape[1], halo.shape[3]
    pairs, rows, _ = sub_ref.shape
    width = 2 * margin
    inner, innermost = sub_in.shape[1], ger_in.shape[1]
    order = [(i, j) for i in range(comps) for j in range(i, comps)]
    outs = []

    def leave(source, target):
        copy = pltpu.make_async_copy(source, target, sems.at[len(outs)])
        copy.start()
        outs.append(copy)

    for p in range(pairs):
        leave(sub_in.at[p], sub_ref.at[p, pl.ds(margin, inner), :])
        leave(ger_in.at[p], ger_ref.at[p, pl.ds(width, innermost), :])

    lane = lax.broadcasted_iota(jnp.int32, (SUB, LANES), 1)

    def ends(side, c):
        up, down = corners[2 + side, c], corners[side, c]
        blocks = []
        for q in range(width // SUB):
            low = pltpu.roll(up, (LANES - q * width) % LANES, 1)
            high = pltpu.roll(down, (LANES - (q + 1) * width) % LANES, 1)
            blocks.append(jnp.where(lane < width, low, jnp.where(lane >= LANES - width, high, 0.0)))
        return jnp.concatenate([halo[side, c], jnp.concatenate(blocks, axis=0)], axis=1)

    def filtered(values, main, edge=None):
        parts = []
        y_filter(stacked(values), margin, cols, main, lambda z, lanes: parts.append(z), edge)
        high, low = split(parts[0] if edge is None else jnp.concatenate(parts, axis=1))
        size = values[0].shape[0]
        return [(high[n * size:(n + 1) * size], low[n * size:(n + 1) * size]) for n in range(len(values))]

    def window(side, late, high, low):
        h = (late[0], high) if side == 0 else (high, late[0])
        l = (late[1], low) if side == 0 else (low, late[1])
        return stacked((h + l) * 2)

    both = [(c, side) for c in range(comps) for side in range(2)]
    every = [(p, side) for p in range(pairs) for side in range(2)]
    ext = {key: ends(key[1], key[0]) for key in both}
    late = filtered([ext[key] for key in both], gym, gye)
    coarse = {}
    for (c, side), z in zip(both, late):
        coarse[c, side] = dot(gxe[...], window(side, z, z1h[c, side], z1l[c, side]))
    at = (slice(width - margin, width), slice(0, margin))
    late = filtered([ext[order[p][0], side][at[side]] * ext[order[p][1], side][at[side]] for p, side in every], gym)
    for (p, side), z in zip(every, late):
        weights = gxe[0:margin] if side == 0 else gxe[width - margin:width]
        value = dot(weights, window(side, z, zph[p, side], zpl[p, side]))
        i, j = order[p]
        sub_e[p, side] = value - coarse[i, side][at[side], 0:cols] * coarse[j, side][at[side], 0:cols]
    leave(sub_e.at[:, 0], sub_ref.at[:, pl.ds(0, margin), :])
    leave(sub_e.at[:, 1], sub_ref.at[:, pl.ds(rows - margin, margin), :])
    late = filtered([coarse[key] for key in both]
                    + [coarse[order[p][0], side] * coarse[order[p][1], side] for p, side in every], tym)
    tested = {}
    for (c, side), z in zip(both, late):
        tested[c, side] = dot(txe[...], window(side, z, z2h[c, side], z2l[c, side]))
    for (p, side), z in zip(every, late[len(both):]):
        value = dot(txe[...], window(side, z, z2h[comps + p, side], z2l[comps + p, side]))
        i, j = order[p]
        ger_e[p, side] = value - tested[i, side] * tested[j, side]
    leave(ger_e.at[:, 0], ger_ref.at[:, pl.ds(0, width), :])
    leave(ger_e.at[:, 1], ger_ref.at[:, pl.ds(rows - width, width), :])
    for copy in outs:
        copy.wait()


def local(nx, ny, velocity, grid_x, grid_y, test_x, test_y):
    comps, planes, cols, rows = velocity.shape
    taps = grid_x.shape[0]
    margin = (taps - 1) // 2
    width = 2 * margin
    wide = cols + LANES
    step = LANES - width
    pairs = comps * (comps + 1) // 2
    batch = 2
    slots = max(comps, 2 * batch)
    vmem = pl.BlockSpec(memory_space=pltpu.VMEM)
    anywhere = pl.BlockSpec(memory_space=pl.ANY)
    packed = rows // width * SUB
    inner, innermost = rows - width, rows - 2 * width
    filled = max((n + step - 1) // step * step + width for n in (inner, innermost))
    fields = comps + pairs
    subs, gers = [], []
    shape = jax.ShapeDtypeStruct
    for plane in range(planes):
        v = jnp.swapaxes(velocity[:, plane], 1, 2)
        parts = pl.pallas_call(
            functools.partial(interior_kernel, nx, ny, width, batch),
            out_shape=(
                shape((2, comps, width, cols), F32),
                shape((4, comps, SUB, LANES), F32),
                shape((comps, 2, width, wide), BF),
                shape((comps, 2, width, wide), BF),
                shape((pairs, 2, width + margin, cols), BF),
                shape((pairs, 2, width + margin, cols), BF),
                shape((fields, 2, width, cols), BF),
                shape((fields, 2, width, cols), BF),
                shape((pairs, inner, cols), F32),
                shape((pairs, innermost, cols), F32),
                shape((width, 2 * LANES), BF),
                shape((width, 2 * LANES), BF),
                shape((3 * cols + LANES, cols), BF),
                shape((3 * LANES, LANES), BF),
                shape((3 * cols + LANES, cols), BF),
            ),
            in_specs=[pl.BlockSpec(memory_space=pltpu.HBM)] * 5,
            out_specs=(vmem,) * 15,
            scratch_shapes=[
                pltpu.VMEM((comps, rows, wide), F32),
                pltpu.VMEM((comps, rows, cols), F32),
                pltpu.VMEM((taps, cols), F32),
                pltpu.VMEM((1, taps), F32),
                pltpu.VMEM((1, taps), F32),
                pltpu.VMEM((taps, cols), F32),
                pltpu.VMEM((round_up(taps, SUB), wide), F32),
                pltpu.VMEM((2 * step, 2 * LANES), BF),
                pltpu.VMEM((2 * step, 2 * LANES), BF),
                pltpu.VMEM((comps, packed, LANES), F32),
                pltpu.VMEM((comps, packed, LANES), F32),
                pltpu.VMEM((comps, packed, LANES), F32),
                pltpu.VMEM((comps, packed, LANES), F32),
                pltpu.VMEM((taps, LANES), F32),
                pltpu.VMEM((taps, LANES), F32),
                pltpu.VMEM((comps, inner, wide), F32),
                pltpu.VMEM((comps, innermost, cols), F32),
                pltpu.VMEM((slots, max(rows, filled), wide), BF),
                pltpu.VMEM((slots, max(rows, filled), wide), BF),
                pltpu.SemaphoreType.DMA((5,)),
                pltpu.SemaphoreType.DMA((len(DIRECTIONS) + 2,)),
                pltpu.SemaphoreType.DMA((len(DIRECTIONS) + 2,)),
                pltpu.SemaphoreType.REGULAR,
            ],
            compiler_params=pltpu.CompilerParams(
                collective_id=plane, has_side_effects=True, vmem_limit_bytes=48 << 20),
            name="interior",
        )(*[pltpu.with_memory_space_constraint(x, pltpu.HBM) for x in (
            v, grid_y.T, grid_x.reshape(1, taps), test_x.reshape(1, taps), test_y.T)])
        out = shape((pairs, rows, cols), F32)
        sub, ger = pl.pallas_call(
            functools.partial(edge_kernel, margin),
            out_shape=(out, out),
            in_specs=[vmem] * 15,
            out_specs=(anywhere, anywhere),
            scratch_shapes=[
                pltpu.VMEM((pairs, 2, margin, cols), F32),
                pltpu.VMEM((pairs, 2, width, cols), F32),
                pltpu.SemaphoreType.DMA((2 * pairs + 4,)),
            ],
            compiler_params=pltpu.CompilerParams(vmem_limit_bytes=48 << 20),
            name="edge",
        )(*parts)
        subs.append(jnp.swapaxes(sub, 1, 2))
        gers.append(jnp.swapaxes(ger, 1, 2))
    return jnp.stack(subs, axis=1), jnp.stack(gers, axis=1)


def solution(mesh):
    nx, ny = mesh.shape["gx"], mesh.shape["gy"]
    field = P(None, None, "gy", "gx")
    return jax.shard_map(
        functools.partial(local, nx, ny),
        mesh=mesh,
        in_specs=(field, P(), P("gy", None), P(), P("gy", None)),
        out_specs=(field, field),
        check_vma=False,
    )
```

time: 22 us -> 19.7 us (0.90)
  the two profiles are of different devices: /device:TPU:0 before, /device:TPU:1 now
where the time goes in v1:
time: 19.7 us; the launch traced here: 19.5 us
  Pallas kernels  18.9 us (96%)
  between operations  0.64 us (3%)
    pallas_call x1, Pallas kernels, local(): pl.pallas_call(functools.partial(interior_kernel, nx, ny, width, batch),...  15 us
    pallas_call x1, Pallas kernels, local(): pl.pallas_call(functools.partial(edge_kernel, margin), out_shape=(out, ou...  3.91 us

profile of v1, /device:TPU:1, one launch (start us, length us, event | category | flops | bytes accessed | tf_op | source)
XLA Modules:
  0.0 19.5 jit_solution(8758178368232686348)
XLA Ops:
  0.6 15.0 %interior.1 = (f32[2,3,32,256]{3,2,1,0:T(8,128)S(1)}, f32[4,3,8,128]{3,2,1,0:T(8,128)S(1)}, bf16[3,2,32,384]{3,2,1,0:T(8,128)(2,1)S(1)}, bf16[3,2,32,384]{3,2,1,...) custom-call(f32[3,320,256]{2,1,0:T(8,128)} %bitcast.17, ...), custom_call_target="tpu_custom_call" | custom-call | tf_op jit(solution)/shard_map/interior/pallas_call | solution.py:428
  15.6 3.9 %edge.1 = (f32[6,320,256]{2,1,0:T(8,128)}, f32[6,320,256]{2,1,0:T(8,128)}) custom-call(f32[2,3,32,256]{3,2,1,0:T(8,128)S(1)} %get-tuple-element.19.halo, f32[4,3,8,128]{3,2,1,0:T(8,128)S(1)} %get-tuple-element.20.corners, bf16[3,2,32,384]{3,2,1,0:T(8,128)(2,1)S(1)} %get-tuple-element.21.z1h, bf16[3,2,32,384]{3,2,1,0:T(8,128)(2,1)S(1)} %get-tuple-element.22.z1l, ...), custom_call_target="tpu_custom_call" | custom-call | tf_op jit(solution)/shard_map/edge/pallas_call | solution.py:480

commit v2 on v1

--- a/solution.py
+++ b/solution.py
@@ -10,7 +10,6 @@
 MESH = pl.DeviceIdType.MESH
 LANES = 128
 SUB = 8
-DIRECTIONS = [(1, 0), (-1, 0), (0, 1), (0, -1), (1, 1), (-1, 1), (1, -1), (-1, -1)]
 BF = jnp.bfloat16
 F32 = jnp.float32
 
@@ -44,11 +43,11 @@
     out[0:step, LANES:] = high
     out[step:, 0:LANES] = low
     out[step:, LANES:] = jnp.zeros((step, LANES), BF)
-    width = edge.shape[0]
+    width = edge.shape[0] // 2
     high, low = split(band[0:width])
     high = high.astype(F32)
-    edge[:, 0:LANES] = (high + pltpu.roll(high, 2 * width, 1)).astype(BF)
-    edge[:, LANES:] = low
+    edge[0:width] = (high + pltpu.roll(high, 2 * width, 1)).astype(BF)
+    edge[width:] = low
 
 
 def y_weights(table, taps, first_row, total, cols, main, edge=None, tiles=None):
@@ -90,21 +89,42 @@
             edge[2 * LANES:] = low
 
 
-def y_filter(value, margin, cols, main, put, edge=None):
+def y_own(value, cols, main):
+    high, low = split(value)
+    return dot(jnp.concatenate([high, high, low], axis=1), main[0:3 * cols])
+
+
+def packed_halo(halo, margin):
+    lane = lax.broadcasted_iota(jnp.int32, halo.shape, 1)
+    near = jnp.where((lane < margin) | (lane >= LANES - margin), halo, 0.0)
+    high = near.astype(BF).astype(F32)
+    return (high + pltpu.roll(near - high, 2 * margin, 1) + pltpu.roll(high, 4 * margin, 1)).astype(BF)
+
+
+def y_halo(halo, margin, cols, main):
+    return dot(packed_halo(halo, margin), main[3 * cols:])
+
+
+def y_filter(value, margin, cols, main):
     high, low = split(value[:, 0:cols])
+    return dot(jnp.concatenate([high, high, low, packed_halo(value[:, cols:], margin)], axis=1), main[...])
+
+
+def y_ends(value, margin, cols, edge):
+    width = 2 * margin
     halo = value[:, cols:]
     lane = lax.broadcasted_iota(jnp.int32, halo.shape, 1)
-    near = jnp.where((lane < margin) | (lane >= LANES - margin), halo, 0.0)
-    near_high = near.astype(BF).astype(F32)
-    packed = near_high + pltpu.roll(near - near_high, 2 * margin, 1) + pltpu.roll(near_high, 4 * margin, 1)
-    put(dot(jnp.concatenate([high, high, low, packed.astype(BF)], axis=1), main[...]), slice(0, cols))
-    if edge is not None:
-        width = 2 * margin
-        own = jnp.where(lane < LANES // 2, pltpu.roll(value[:, 0:LANES], width, 1),
-                        pltpu.roll(value[:, cols - LANES:cols], LANES - width, 1))
-        ends = jnp.where((lane < width) | (lane >= LANES - width), halo, own)
-        high, low = split(ends)
-        put(dot(jnp.concatenate([high, low, high], axis=1), edge[...]), slice(cols, cols + LANES))
+    own = jnp.where(lane < LANES // 2, pltpu.roll(value[:, 0:LANES], width, 1),
+                    pltpu.roll(value[:, cols - LANES:cols], LANES - width, 1))
+    high, low = split(jnp.where((lane < width) | (lane >= LANES - width), halo, own))
+    return dot(jnp.concatenate([high, low, high], axis=1), edge[...])
+
+
+def side_lanes(up, down, q, width):
+    lane = lax.broadcasted_iota(jnp.int32, up.shape, 1)
+    low = pltpu.roll(up, (LANES - q * width) % LANES, 1)
+    high = pltpu.roll(down, (LANES - (q + 1) * width) % LANES, 1)
+    return jnp.where(lane < width, low, jnp.where(lane >= LANES - width, high, 0.0))
 
 
 def x_filter(zh, zl, start, count, lanes, weights, put):
@@ -126,11 +146,11 @@
 
 def interior_kernel(nx, ny, width, batch, v_hbm, t_hbm, gx_hbm, tx_hbm, ty_hbm,
                     halo, corners, z1h, z1l, zph, zpl, z2h, z2l, sub, ger, gxe, txe, gym, gye, tym,
-                    ext, v_ref, t_ref, gx_ref, tx_ref, ty_ref, text_ref, gxw, txw,
+                    ext, t_ref, gx_ref, tx_ref, ty_ref, text_ref, gxw, txw,
                     pack_d, pack_u, from_d, from_u, t_low, t_high,
-                    coarse, tested, zh, zl, load_sem, send_sem, recv_sem, ready):
-    comps, rows, cols = v_ref.shape
-    taps = t_ref.shape[0]
+                    own_v, own_p, coarse, tested, zh, zl, load_sem, send_sem, recv_sem, ready):
+    comps, rows, _ = ext.shape
+    taps, cols = t_ref.shape
     margin = width // 2
     pairs, inner, _ = sub.shape
     innermost = ger.shape[1]
@@ -158,45 +178,74 @@
 
         pl.when(present & not_last)(lambda sign=sign: signal(barrier, 1, sign))
 
+    own = slice(0, cols)
+    everything = slice(0, cols + LANES)
     loads = [pltpu.make_async_copy(src, dst, load_sem.at[i]) for i, (src, dst) in enumerate((
-        (v_hbm, v_ref), (t_hbm, t_ref), (gx_hbm, gx_ref), (tx_hbm, tx_ref), (ty_hbm, ty_ref)))]
+        (t_hbm, t_ref), (gx_hbm, gx_ref), (tx_hbm, tx_ref), (ty_hbm, ty_ref),
+        (v_hbm, ext.at[:, :, own])))]
     for load in loads:
         load.start()
+
+    text_ref[...] = jnp.zeros_like(text_ref)
+    filled = zh.shape[1]
+    for slot in range(zh.shape[0]):
+        zh[slot, inner:filled, :] = jnp.zeros((filled - inner, cols + LANES), BF)
+        zl[slot, inner:filled, :] = jnp.zeros((filled - inner, cols + LANES), BF)
+    for sign, present, mid in ((1, has_up, from_u), (-1, has_down, from_d)):
+        @pl.when(jnp.logical_not(present))
+        def _(sign=sign, mid=mid):
+            mid[...] = jnp.zeros_like(mid)
+            for side in range(2):
+                corners[side + (2 if sign > 0 else 0)] = jnp.zeros(corners.shape[1:], F32)
+
+    for load in loads[:4]:
+        load.wait()
+    text_ref[0:taps, 0:cols] = t_ref[...]
+    first_row, total = me_y * cols, cols * ny
+    own_tiles = range(cols // LANES)
+    y_weights(t_ref[...], taps, first_row, total, cols, gym, tiles=own_tiles)
+
     per = LANES // width
     groups = rows // width
-    loads[0].wait()
+    loads[4].wait()
     for c in range(comps):
         for g in range(groups):
             for q in range(per):
                 src = pl.ds(g * width + q * SUB, SUB)
                 dst = pl.ds(g * SUB, SUB)
-                pack_u[c, dst, q * width:(q + 1) * width] = v_ref[c, src, cols - width:cols]
-                pack_d[c, dst, q * width:(q + 1) * width] = v_ref[c, src, 0:width]
+                pack_u[c, dst, q * width:(q + 1) * width] = ext[c, src, cols - width:cols]
+                pack_d[c, dst, q * width:(q + 1) * width] = ext[c, src, 0:width]
     pl.semaphore_wait(barrier, 1 + 2 * vertical + jnp.where(first, 0, 1 + vertical))
 
     head, tail = pl.ds(0, SUB), pl.ds((groups - 1) * SUB, SUB)
-    sources = [
-        v_hbm.at[:, pl.ds(rows - width, width), :], v_hbm.at[:, pl.ds(0, width), :],
-        pack_u, pack_d,
-        pack_u.at[:, tail, :], pack_u.at[:, head, :], pack_d.at[:, tail, :], pack_d.at[:, head, :],
-    ]
-    targets = [halo.at[0], halo.at[1], from_d, from_u] + [corners.at[i] for i in range(4)]
+    low_x, high_x = v_hbm.at[:, pl.ds(0, width), :], v_hbm.at[:, pl.ds(rows - width, width), :]
     copies = {}
-    for i, where in enumerate(DIRECTIONS):
-        copies[where] = pltpu.make_async_remote_copy(
-            src_ref=sources[i], dst_ref=targets[i], send_sem=send_sem.at[i],
-            recv_sem=recv_sem.at[i], device_id=device(*where), device_id_type=MESH)
-    tables = {}
-    for i, (sign, src, dst) in enumerate((
-        (1, t_ref.at[:, pl.ds(cols - LANES, LANES)], t_low),
-        (-1, t_ref.at[:, pl.ds(0, LANES)], t_high),
-    )):
-        n = len(DIRECTIONS) + i
-        tables[sign] = pltpu.make_async_remote_copy(
-            src_ref=src, dst_ref=dst, send_sem=send_sem.at[n],
-            recv_sem=recv_sem.at[n], device_id=device(0, sign), device_id_type=MESH)
-
-    copies[1, 0].start()
+
+    def remote(key, src, dst, dx, dy):
+        n = len(copies)
+        copies[key] = pltpu.make_async_remote_copy(
+            src_ref=src, dst_ref=dst, send_sem=send_sem.at[n], recv_sem=recv_sem.at[n],
+            device_id=device(dx, dy), device_id_type=MESH)
+
+    remote((1, 0), high_x, halo.at[0], 1, 0)
+    remote((-1, 0), low_x, halo.at[1], -1, 0)
+    remote((1, 1), pack_u.at[:, tail, :], corners.at[0], 1, 1)
+    remote((-1, 1), pack_u.at[:, head, :], corners.at[1], -1, 1)
+    remote((1, -1), pack_d.at[:, tail, :], corners.at[2], 1, -1)
+    remote((-1, -1), pack_d.at[:, head, :], corners.at[3], -1, -1)
+    remote(("t", 1), t_ref.at[:, pl.ds(cols - LANES, LANES)], t_low, 0, 1)
+    remote(("t", -1), t_ref.at[:, pl.ds(0, LANES)], t_high, 0, -1)
+    for c in range(comps):
+        remote((c, "v", 1), pack_u.at[c], from_d.at[c], 0, 1)
+        remote((c, "v", -1), pack_d.at[c], from_u.at[c], 0, -1)
+
+    pl.when(last)(lambda: copies[1, 0].start())
+    for sign, present in sides:
+        @pl.when(present)
+        def _(sign=sign):
+            copies["t", sign].start()
+            for c in range(comps):
+                copies[c, "v", sign].start()
 
     @pl.when(last)
     def _():
@@ -204,82 +253,62 @@
         for sign, present in sides:
             pl.when(present)(lambda sign=sign: signal(ready, 1, sign))
 
+    pl.when(not_last)(lambda: copies[1, 0].start())
     pl.when(not_first)(lambda: copies[-1, 0].start())
-    loads[1].wait()
     for sign, present in sides:
-        @pl.when(present)
-        def _(sign=sign):
-            copies[0, sign].start()
-            tables[sign].start()
-            copies[1, sign].start()
-
+        pl.when(present)(lambda sign=sign: copies[1, sign].start())
         pl.when(present & not_first)(lambda sign=sign: copies[-1, sign].start())
 
-    ext[:, :, cols:] = jnp.zeros((comps, rows, LANES), F32)
-    text_ref[...] = jnp.zeros_like(text_ref)
-    for sign, present in sides:
-        @pl.when(jnp.logical_not(present))
-        def _(sign=sign):
-            for side in range(2):
-                corners[side + (2 if sign > 0 else 0)] = jnp.zeros(corners.shape[1:], F32)
-
     for c in range(comps):
-        ext[c, :, 0:cols] = v_ref[c]
-    text_ref[0:taps, 0:cols] = t_ref[...]
-    for load in loads[2:]:
-        load.wait()
-    first_row, total = me_y * cols, cols * ny
+        own_v[c] = y_own(ext[c, :, own], cols, gym)
+
+    @pl.loop(0, pairs // batch)
+    def _(step):
+        indices = [(step * batch + b,) + pair_of(step * batch + b) for b in range(batch)]
+        z = y_own(stacked([ext[i, :, own] * ext[j, :, own] for _, i, j in indices]), cols, gym)
+        for b, (p, _, _) in enumerate(indices):
+            own_p[p] = z[b * rows:(b + 1) * rows]
+
     x_weights(gx_ref, gxw.shape[0] // 2, gxw, gxe)
     x_weights(tx_ref, txw.shape[0] // 2, txw, txe)
-    own_tiles = range(cols // LANES)
-    y_weights(t_ref[...], taps, first_row, total, cols, gym, tiles=own_tiles)
     y_weights(ty_ref[...], taps, first_row, total, cols, tym, tiles=own_tiles)
-    filled = zh.shape[1]
-    for slot in range(zh.shape[0]):
-        zh[slot, inner:filled, :] = jnp.zeros((filled - inner, cols + LANES), BF)
-        zl[slot, inner:filled, :] = jnp.zeros((filled - inner, cols + LANES), BF)
-
-    for sign, present, lane, mid, tile, at in (
-        (1, has_down, cols + LANES - width, from_d, t_low, LANES - margin),
-        (-1, has_up, cols, from_u, t_high, 0),
-    ):
+
+    for sign, present, tile, at in ((1, has_down, t_low, LANES - margin), (-1, has_up, t_high, 0)):
         @pl.when(present)
-        def _(sign=sign, lane=lane, mid=mid, tile=tile, at=at):
-            copies[0, sign].wait_recv()
-            tables[sign].wait_recv()
-            for c in range(comps):
-                for g in range(groups):
-                    for q in range(per):
-                        ext[c, pl.ds(g * width + q * SUB, SUB), lane:lane + width] = (
-                            mid[c, pl.ds(g * SUB, SUB), q * width:(q + 1) * width])
+        def _(sign=sign, tile=tile, at=at):
+            copies["t", sign].wait_recv()
             text_ref[0:taps, cols + at:cols + at + margin] = tile[:, at:at + margin]
 
     y_weights(text_ref[...], taps, first_row, total, cols, gym, gye, tiles=(cols // LANES,))
 
-    own = slice(0, cols)
-    everything = slice(0, cols + LANES)
-
-    def store(slot, n, count):
-        def put(z, lanes):
-            high, low = split(z)
-            for b in range(n):
-                at = slice(b * count, (b + 1) * count)
-                zh[slot + b, 0:count, lanes], zl[slot + b, 0:count, lanes] = high[at], low[at]
-        return put
+    def store(slot, count, lanes, z):
+        high, low = split(z)
+        for b in range(z.shape[0] // count):
+            at = slice(b * count, (b + 1) * count)
+            zh[slot + b, 0:count, lanes], zl[slot + b, 0:count, lanes] = high[at], low[at]
 
     def keep(slot, count, size, lanes, high, low, index):
         for side, at in enumerate((slice(0, size), slice(count - size, count))):
             high[index, side] = zh[slot, at, lanes]
             low[index, side] = zl[slot, at, lanes]
 
-    y_filter(stacked([ext[c] for c in range(comps)]), margin, cols, gym, store(0, comps, rows), gye)
     for c in range(comps):
+        for sign, present in ((1, has_down), (-1, has_up)):
+            pl.when(present)(lambda sign=sign, c=c: copies[c, "v", sign].wait_recv())
+        for g in range(groups):
+            at = pl.ds(g * SUB, SUB)
+            up, down = from_u[c, at, :], from_d[c, at, :]
+            for q in range(per):
+                ext[c, pl.ds(g * width + q * SUB, SUB), cols:] = side_lanes(up, down, q, width)
+        store(c, rows, own, own_v[c] + y_halo(ext[c, :, cols:], margin, cols, gym))
+        store(c, rows, slice(cols, cols + LANES), y_ends(ext[c], margin, cols, gye))
+
         def put(start, size, value, c=c):
             coarse[c, pl.ds(start, size), :] = value
 
         x_filter(zh.at[c], zl.at[c], 0, inner, everything, gxw, put)
         keep(c, rows, width, everything, z1h, z1l, c)
-    y_filter(stacked([coarse[c] for c in range(comps)]), margin, cols, tym, store(0, comps, inner))
+    store(0, inner, own, y_filter(stacked([coarse[c] for c in range(comps)]), margin, cols, tym))
     for c in range(comps):
         def put_tested(start, size, value, c=c):
             tested[c, pl.ds(start, size), :] = value
@@ -297,9 +326,10 @@
     @pl.loop(0, pairs // batch)
     def _(step):
         indices = [(step * batch + b,) + pair_of(step * batch + b) for b in range(batch)]
-        y_filter(stacked([ext[i] * ext[j] for _, i, j in indices]), margin, cols, gym, store(0, batch, rows))
-        y_filter(stacked([coarse[i] * coarse[j] for _, i, j in indices]),
-                 margin, cols, tym, store(batch, batch, inner))
+        halos = y_halo(stacked([ext[i, :, cols:] * ext[j, :, cols:] for _, i, j in indices]), margin, cols, gym)
+        store(0, rows, own, stacked([own_p[p] for p, _, _ in indices]) + halos)
+        store(batch, inner, own,
+              y_filter(stacked([coarse[i] * coarse[j] for _, i, j in indices]), margin, cols, tym))
         for b, (p, i, j) in enumerate(indices):
             def put_sub(start, size, value, p=p, i=i, j=j):
                 at = pl.ds(start, size)
@@ -328,9 +358,11 @@
     for sign, present in sides:
         @pl.when(present)
         def _(sign=sign):
-            for dx in (0, 1, -1):
-                copies[dx, sign].wait_send()
-            tables[sign].wait_send()
+            copies[1, sign].wait_send()
+            copies[-1, sign].wait_send()
+            copies["t", sign].wait_send()
+            for c in range(comps):
+                copies[c, "v", sign].wait_send()
 
 
 def edge_kernel(margin, halo, corners, z1h, z1l, zph, zpl, z2h, z2l, sub_in, ger_in,
@@ -351,52 +383,52 @@
         leave(sub_in.at[p], sub_ref.at[p, pl.ds(margin, inner), :])
         leave(ger_in.at[p], ger_ref.at[p, pl.ds(width, innermost), :])
 
-    lane = lax.broadcasted_iota(jnp.int32, (SUB, LANES), 1)
-
     def ends(side, c):
         up, down = corners[2 + side, c], corners[side, c]
-        blocks = []
-        for q in range(width // SUB):
-            low = pltpu.roll(up, (LANES - q * width) % LANES, 1)
-            high = pltpu.roll(down, (LANES - (q + 1) * width) % LANES, 1)
-            blocks.append(jnp.where(lane < width, low, jnp.where(lane >= LANES - width, high, 0.0)))
+        blocks = [side_lanes(up, down, q, width) for q in range(width // SUB)]
         return jnp.concatenate([halo[side, c], jnp.concatenate(blocks, axis=0)], axis=1)
 
-    def filtered(values, main, edge=None):
-        parts = []
-        y_filter(stacked(values), margin, cols, main, lambda z, lanes: parts.append(z), edge)
-        high, low = split(parts[0] if edge is None else jnp.concatenate(parts, axis=1))
-        size = values[0].shape[0]
-        return [(high[n * size:(n + 1) * size], low[n * size:(n + 1) * size]) for n in range(len(values))]
-
-    def window(side, late, high, low):
+    def pieces(z, size, count):
+        high, low = split(z)
+        return [(high[n * size:(n + 1) * size], low[n * size:(n + 1) * size]) for n in range(count)]
+
+    def x_ends(side, late, high, low, weights):
         h = (late[0], high) if side == 0 else (high, late[0])
         l = (late[1], low) if side == 0 else (low, late[1])
-        return stacked((h + l) * 2)
+        r = dot(weights, stacked(h + l))
+        half = weights.shape[0] // 2
+        return r[0:half] + r[half:]
 
     both = [(c, side) for c in range(comps) for side in range(2)]
     every = [(p, side) for p in range(pairs) for side in range(2)]
+    near = (slice(width - margin, width), slice(0, margin))
     ext = {key: ends(key[1], key[0]) for key in both}
-    late = filtered([ext[key] for key in both], gym, gye)
+    values = stacked([ext[key] for key in both])
+    products = stacked([ext[order[p][0], side][near[side]] * ext[order[p][1], side][near[side]] for p, side in every])
+    z = y_filter(stacked([values, products]), margin, cols, gym)
+    count = len(both) * width
+    late = pieces(jnp.concatenate([z[0:count], y_ends(values, margin, cols, gye)], axis=1), width, len(both))
     coarse = {}
-    for (c, side), z in zip(both, late):
-        coarse[c, side] = dot(gxe[...], window(side, z, z1h[c, side], z1l[c, side]))
-    at = (slice(width - margin, width), slice(0, margin))
-    late = filtered([ext[order[p][0], side][at[side]] * ext[order[p][1], side][at[side]] for p, side in every], gym)
-    for (p, side), z in zip(every, late):
-        weights = gxe[0:margin] if side == 0 else gxe[width - margin:width]
-        value = dot(weights, window(side, z, zph[p, side], zpl[p, side]))
+    for (c, side), part in zip(both, late):
+        coarse[c, side] = x_ends(side, part, z1h[c, side], z1l[c, side], gxe[...])
+    late = pieces(z[count:], margin, len(every))
+    for (p, side), part in zip(every, late):
+        weights = stacked([gxe[0:margin], gxe[width:width + margin]] if side == 0 else
+                          [gxe[width - margin:width], gxe[2 * width - margin:]])
+        value = x_ends(side, part, zph[p, side], zpl[p, side], weights)
         i, j = order[p]
-        sub_e[p, side] = value - coarse[i, side][at[side], 0:cols] * coarse[j, side][at[side], 0:cols]
+        sub_e[p, side] = value - coarse[i, side][near[side], 0:cols] * coarse[j, side][near[side], 0:cols]
     leave(sub_e.at[:, 0], sub_ref.at[:, pl.ds(0, margin), :])
     leave(sub_e.at[:, 1], sub_ref.at[:, pl.ds(rows - margin, margin), :])
-    late = filtered([coarse[key] for key in both]
-                    + [coarse[order[p][0], side] * coarse[order[p][1], side] for p, side in every], tym)
+    z = y_filter(stacked([coarse[key] for key in both]
+                         + [coarse[order[p][0], side] * coarse[order[p][1], side] for p, side in every]),
+                 margin, cols, tym)
+    late = pieces(z, width, len(both) + len(every))
     tested = {}
-    for (c, side), z in zip(both, late):
-        tested[c, side] = dot(txe[...], window(side, z, z2h[c, side], z2l[c, side]))
-    for (p, side), z in zip(every, late[len(both):]):
-        value = dot(txe[...], window(side, z, z2h[comps + p, side], z2l[comps + p, side]))
+    for (c, side), part in zip(both, late):
+        tested[c, side] = x_ends(side, part, z2h[c, side], z2l[c, side], txe[...])
+    for (p, side), part in zip(every, late[len(both):]):
+        value = x_ends(side, part, z2h[comps + p, side], z2l[comps + p, side], txe[...])
         i, j = order[p]
         ger_e[p, side] = value - tested[i, side] * tested[j, side]
     leave(ger_e.at[:, 0], ger_ref.at[:, pl.ds(0, width), :])
@@ -438,8 +470,8 @@
                 shape((fields, 2, width, cols), BF),
                 shape((pairs, inner, cols), F32),
                 shape((pairs, innermost, cols), F32),
-                shape((width, 2 * LANES), BF),
-                shape((width, 2 * LANES), BF),
+                shape((2 * width, LANES), BF),
+                shape((2 * width, LANES), BF),
                 shape((3 * cols + LANES, cols), BF),
                 shape((3 * LANES, LANES), BF),
                 shape((3 * cols + LANES, cols), BF),
@@ -448,7 +480,6 @@
             out_specs=(vmem,) * 15,
             scratch_shapes=[
                 pltpu.VMEM((comps, rows, wide), F32),
-                pltpu.VMEM((comps, rows, cols), F32),
                 pltpu.VMEM((taps, cols), F32),
                 pltpu.VMEM((1, taps), F32),
                 pltpu.VMEM((1, taps), F32),
@@ -462,13 +493,15 @@
                 pltpu.VMEM((comps, packed, LANES), F32),
                 pltpu.VMEM((taps, LANES), F32),
                 pltpu.VMEM((taps, LANES), F32),
+                pltpu.VMEM((comps, rows, cols), F32),
+                pltpu.VMEM((pairs, rows, cols), F32),
                 pltpu.VMEM((comps, inner, wide), F32),
                 pltpu.VMEM((comps, innermost, cols), F32),
                 pltpu.VMEM((slots, max(rows, filled), wide), BF),
                 pltpu.VMEM((slots, max(rows, filled), wide), BF),
                 pltpu.SemaphoreType.DMA((5,)),
-                pltpu.SemaphoreType.DMA((len(DIRECTIONS) + 2,)),
-                pltpu.SemaphoreType.DMA((len(DIRECTIONS) + 2,)),
+                pltpu.SemaphoreType.DMA((8 + 2 * comps,)),
+                pltpu.SemaphoreType.DMA((8 + 2 * comps,)),
                 pltpu.SemaphoreType.REGULAR,
             ],
             compiler_params=pltpu.CompilerParams(

time: 19.7 us -> 17.6 us (0.89)
  Pallas kernels: 18.9 us -> 16.8 us
    pallas_call x1, Pallas kernels: 15 us -> 13.3 us  [local(): pl.pallas_call(functools.partial(interior_kernel, nx, ny, width, batch),...]
    pallas_call x1, Pallas kernels: 3.91 us -> 3.49 us  [local(): pl.pallas_call(functools.partial(edge_kernel, margin), out_shape=(out, ou...]
where the time goes in v2:
time: 17.6 us; the launch traced here: 17.5 us
  Pallas kernels  16.8 us (95%)
  between operations  0.64 us (4%)
    pallas_call x1, Pallas kernels, local(): pl.pallas_call(functools.partial(interior_kernel, nx, ny, width, batch),...  13.3 us
    pallas_call x1, Pallas kernels, local(): pl.pallas_call(functools.partial(edge_kernel, margin), out_shape=(out, ou...  3.49 us

profile of v2, /device:TPU:1, one launch (start us, length us, event | category | flops | bytes accessed | tf_op | source)
XLA Modules:
  0.0 17.5 jit_solution(9178880496698459747)
XLA Ops:
  0.6 13.3 %interior.1 = (f32[2,3,32,256]{3,2,1,0:T(8,128)S(1)}, f32[4,3,8,128]{3,2,1,0:T(8,128)S(1)}, bf16[3,2,32,384]{3,2,1,0:T(8,128)(2,1)S(1)}, bf16[3,2,32,384]{3,2,1,...) custom-call(f32[3,320,256]{2,1,0:T(8,128)} %bitcast.17, ...), custom_call_target="tpu_custom_call" | custom-call | tf_op jit(solution)/shard_map/interior/pallas_call | solution.py:460
  14.0 3.5 %edge.1 = (f32[6,320,256]{2,1,0:T(8,128)}, f32[6,320,256]{2,1,0:T(8,128)}) custom-call(f32[2,3,32,256]{3,2,1,0:T(8,128)S(1)} %get-tuple-element.19.halo, f32[4,3,8,128]{3,2,1,0:T(8,128)S(1)} %get-tuple-element.20.corners, bf16[3,2,32,384]{3,2,1,0:T(8,128)(2,1)S(1)} %get-tuple-element.21.z1h, bf16[3,2,32,384]{3,2,1,0:T(8,128)(2,1)S(1)} %get-tuple-element.22.z1l, ...), custom_call_target="tpu_custom_call" | custom-call | tf_op jit(solution)/shard_map/edge/pallas_call | solution.py:513

commit v3 on v2

--- a/solution.py
+++ b/solution.py
@@ -23,12 +23,6 @@
     return high, (value - high.astype(F32)).astype(BF)
 
 
-def pair_of(p):
-    first = jnp.where(p < 3, 0, jnp.where(p < 5, 1, 2))
-    second = jnp.where(p < 3, p, jnp.where(p < 5, p - 2, 2))
-    return first, second
-
-
 def dot(a, b):
     return jnp.dot(a, b, preferred_element_type=F32)
 
@@ -39,10 +33,9 @@
     w = w / jnp.sum(w)
     band = pltpu.roll(jnp.broadcast_to(w, (LANES, LANES)), 0, 1, stride=1, stride_axis=0)
     high, low = split(band[0:step])
-    out[0:step, 0:LANES] = high
-    out[0:step, LANES:] = high
-    out[step:, 0:LANES] = low
-    out[step:, LANES:] = jnp.zeros((step, LANES), BF)
+    out[:, 0:LANES] = high
+    out[:, LANES:2 * LANES] = high
+    out[:, 2 * LANES:] = low
     width = edge.shape[0] // 2
     high, low = split(band[0:width])
     high = high.astype(F32)
@@ -127,28 +120,24 @@
     return jnp.where(lane < width, low, jnp.where(lane >= LANES - width, high, 0.0))
 
 
-def x_filter(zh, zl, start, count, lanes, weights, put):
-    step = weights.shape[0] // 2
+def x_filter(zh, zl, count, weights, put):
+    step = weights.shape[0]
     for s in range(0, count, step):
         size = min(step, count - s)
-        at = slice(start + s, start + s + LANES)
-        data = jnp.concatenate([zh[at, lanes], zl[at, lanes]], axis=0)
-        if size == step:
-            r = dot(weights[...], data)
-        else:
-            r = dot(jnp.concatenate([weights[0:size], weights[step:step + size]], axis=0), data)
-        put(s, size, r[0:size] + r[size:])
+        at = slice(s, s + LANES)
+        high = zh[at]
+        put(slice(s, s + size), dot(weights[0:size], jnp.concatenate([high, zl[at], high], axis=0)))
 
 
 def stacked(values):
     return jnp.concatenate(values, axis=0)
 
 
-def interior_kernel(nx, ny, width, batch, v_hbm, t_hbm, gx_hbm, tx_hbm, ty_hbm,
+def interior_kernel(nx, ny, width, v_hbm, t_hbm, gx_hbm, tx_hbm, ty_hbm,
                     halo, corners, z1h, z1l, zph, zpl, z2h, z2l, sub, ger, gxe, txe, gym, gye, tym,
                     ext, t_ref, gx_ref, tx_ref, ty_ref, text_ref, gxw, txw,
                     pack_d, pack_u, from_d, from_u, t_low, t_high,
-                    own_v, own_p, coarse, tested, zh, zl, load_sem, send_sem, recv_sem, ready):
+                    own_v, own_p, coarse, tested, load_sem, send_sem, recv_sem, ready):
     comps, rows, _ = ext.shape
     taps, cols = t_ref.shape
     margin = width // 2
@@ -156,10 +145,11 @@
     innermost = ger.shape[1]
     me_x, me_y = lax.axis_index("gx"), lax.axis_index("gy")
     first, last = me_x == 0, me_x == nx - 1
+    not_first, not_last = me_x > 0, me_x < nx - 1
     has_up, has_down = me_y < ny - 1, me_y > 0
     vertical = jnp.where(has_up, 1, 0) + jnp.where(has_down, 1, 0)
-    not_first, not_last = me_x > 0, me_x < nx - 1
     sides = ((1, has_up), (-1, has_down))
+    columns = ((0, None), (1, has_up), (-1, has_down))
 
     def device(dx, dy):
         return {"gx": lax.rem(me_x + dx + nx, nx), "gy": lax.rem(me_y + dy + ny, ny)}
@@ -167,56 +157,25 @@
     def signal(sem, dx, dy):
         pl.semaphore_signal(sem, inc=1, device_id=device(dx, dy), device_id_type=MESH)
 
+    def column(condition, act):
+        for dy, present in columns:
+            pl.when(condition if present is None else condition & present)(lambda dy=dy: act(dy))
+
     barrier = pltpu.get_barrier_semaphore()
-    signal(barrier, -1, 0)
-    pl.when(not_last)(lambda: signal(barrier, 1, 0))
-    for sign, present in sides:
-        @pl.when(present)
-        def _(sign=sign):
-            signal(barrier, 0, sign)
-            signal(barrier, -1, sign)
-
-        pl.when(present & not_last)(lambda sign=sign: signal(barrier, 1, sign))
+    pl.when(has_up)(lambda: signal(barrier, 0, 1))
+    column(not_last, lambda dy: signal(barrier, 1, dy))
+    column(first, lambda dy: signal(barrier, -1, dy))
 
     own = slice(0, cols)
-    everything = slice(0, cols + LANES)
+    order = [(i, j) for i in range(comps) for j in range(i, comps)]
     loads = [pltpu.make_async_copy(src, dst, load_sem.at[i]) for i, (src, dst) in enumerate((
         (t_hbm, t_ref), (gx_hbm, gx_ref), (tx_hbm, tx_ref), (ty_hbm, ty_ref),
         (v_hbm, ext.at[:, :, own])))]
     for load in loads:
         load.start()
 
-    text_ref[...] = jnp.zeros_like(text_ref)
-    filled = zh.shape[1]
-    for slot in range(zh.shape[0]):
-        zh[slot, inner:filled, :] = jnp.zeros((filled - inner, cols + LANES), BF)
-        zl[slot, inner:filled, :] = jnp.zeros((filled - inner, cols + LANES), BF)
-    for sign, present, mid in ((1, has_up, from_u), (-1, has_down, from_d)):
-        @pl.when(jnp.logical_not(present))
-        def _(sign=sign, mid=mid):
-            mid[...] = jnp.zeros_like(mid)
-            for side in range(2):
-                corners[side + (2 if sign > 0 else 0)] = jnp.zeros(corners.shape[1:], F32)
-
-    for load in loads[:4]:
-        load.wait()
-    text_ref[0:taps, 0:cols] = t_ref[...]
-    first_row, total = me_y * cols, cols * ny
-    own_tiles = range(cols // LANES)
-    y_weights(t_ref[...], taps, first_row, total, cols, gym, tiles=own_tiles)
-
     per = LANES // width
     groups = rows // width
-    loads[4].wait()
-    for c in range(comps):
-        for g in range(groups):
-            for q in range(per):
-                src = pl.ds(g * width + q * SUB, SUB)
-                dst = pl.ds(g * SUB, SUB)
-                pack_u[c, dst, q * width:(q + 1) * width] = ext[c, src, cols - width:cols]
-                pack_d[c, dst, q * width:(q + 1) * width] = ext[c, src, 0:width]
-    pl.semaphore_wait(barrier, 1 + 2 * vertical + jnp.where(first, 0, 1 + vertical))
-
     head, tail = pl.ds(0, SUB), pl.ds((groups - 1) * SUB, SUB)
     low_x, high_x = v_hbm.at[:, pl.ds(0, width), :], v_hbm.at[:, pl.ds(rows - width, width), :]
     copies = {}
@@ -239,39 +198,77 @@
         remote((c, "v", 1), pack_u.at[c], from_d.at[c], 0, 1)
         remote((c, "v", -1), pack_d.at[c], from_u.at[c], 0, -1)
 
-    pl.when(last)(lambda: copies[1, 0].start())
-    for sign, present in sides:
-        @pl.when(present)
-        def _(sign=sign):
-            copies["t", sign].start()
-            for c in range(comps):
-                copies[c, "v", sign].start()
-
     @pl.when(last)
     def _():
-        signal(ready, 1, 0)
-        for sign, present in sides:
-            pl.when(present)(lambda sign=sign: signal(ready, 1, sign))
-
-    pl.when(not_last)(lambda: copies[1, 0].start())
+        pl.semaphore_wait(barrier, jnp.where(has_down, 1, 0) + jnp.where(first, 0, 1 + vertical) + 1 + vertical)
+        copies[1, 0].start()
+
+    column(last, lambda dy: signal(ready.at[1 - dy], 1, dy))
+
+    text_ref[...] = jnp.zeros_like(text_ref)
+    for z, full in ((z1h, rows), (z1l, rows), (zph, rows), (zpl, rows), (z2h, inner), (z2l, inner)):
+        if z.shape[1] > full:
+            z[:, full:, :] = jnp.zeros((z.shape[0], z.shape[1] - full, z.shape[2]), BF)
+    for sign, present, mid in ((1, has_up, from_u), (-1, has_down, from_d)):
+        @pl.when(jnp.logical_not(present))
+        def _(sign=sign, mid=mid):
+            mid[...] = jnp.zeros_like(mid)
+            for side in range(2):
+                corners[side + (2 if sign > 0 else 0)] = jnp.zeros(corners.shape[1:], F32)
+
+    for load in loads[:4]:
+        load.wait()
+    text_ref[0:taps, 0:cols] = t_ref[...]
+    first_row, total = me_y * cols, cols * ny
+    own_tiles = range(cols // LANES)
+    y_weights(t_ref[...], taps, first_row, total, cols, gym, tiles=own_tiles)
+
+    @pl.when(not_last & (not_first | has_down))
+    def _():
+        pl.semaphore_wait(barrier, jnp.where(has_down, 1, 0) + jnp.where(first, 0, 1 + vertical))
+
     pl.when(not_first)(lambda: copies[-1, 0].start())
-    for sign, present in sides:
-        pl.when(present)(lambda sign=sign: copies[1, sign].start())
-        pl.when(present & not_first)(lambda sign=sign: copies[-1, sign].start())
-
+    pl.when(has_down)(lambda: signal(ready.at[3], 0, -1))
+    column(not_first, lambda dy: signal(ready.at[5 - dy], -1, dy))
+
+    loads[4].wait()
     for c in range(comps):
+        for g in range(groups):
+            for q in range(per):
+                src = pl.ds(g * width + q * SUB, SUB)
+                dst = pl.ds(g * SUB, SUB)
+                pack_u[c, dst, q * width:(q + 1) * width] = ext[c, src, cols - width:cols]
+                pack_d[c, dst, q * width:(q + 1) * width] = ext[c, src, 0:width]
+
+    def wall(sign):
+        copies["t", sign].start()
+        for c in range(comps):
+            copies[c, "v", sign].start()
+
+    own_v[0] = y_own(ext[0, :, own], cols, gym)
+    pl.when(has_down)(lambda: wall(-1))
+    for dy, present in sides:
+        pl.when(last & present)(lambda dy=dy: copies[1, dy].start())
+        pl.when(not_first & present)(lambda dy=dy: copies[-1, dy].start())
+
+    for c in range(1, comps):
         own_v[c] = y_own(ext[c, :, own], cols, gym)
 
-    @pl.loop(0, pairs // batch)
-    def _(step):
-        indices = [(step * batch + b,) + pair_of(step * batch + b) for b in range(batch)]
-        z = y_own(stacked([ext[i, :, own] * ext[j, :, own] for _, i, j in indices]), cols, gym)
-        for b, (p, _, _) in enumerate(indices):
-            own_p[p] = z[b * rows:(b + 1) * rows]
-
-    x_weights(gx_ref, gxw.shape[0] // 2, gxw, gxe)
-    x_weights(tx_ref, txw.shape[0] // 2, txw, txe)
+    @pl.when(has_up)
+    def _():
+        pl.semaphore_wait(ready.at[3], 1)
+        wall(1)
+
+    def forward(dx, dy):
+        pl.semaphore_wait(ready.at[(5 if dx > 0 else 1) + dy], 1)
+        copies[dx, dy].start()
+
+    x_weights(gx_ref, gxw.shape[0], gxw, gxe)
+    x_weights(tx_ref, txw.shape[0], txw, txe)
     y_weights(ty_ref[...], taps, first_row, total, cols, tym, tiles=own_tiles)
+    for p, (i, j) in enumerate(order):
+        own_p[p] = y_own(ext[i, :, own] * ext[j, :, own], cols, gym)
+    column(not_last, lambda dy: forward(1, dy))
 
     for sign, present, tile, at in ((1, has_down, t_low, LANES - margin), (-1, has_up, t_high, 0)):
         @pl.when(present)
@@ -281,69 +278,87 @@
 
     y_weights(text_ref[...], taps, first_row, total, cols, gym, gye, tiles=(cols // LANES,))
 
-    def store(slot, count, lanes, z):
-        high, low = split(z)
-        for b in range(z.shape[0] // count):
-            at = slice(b * count, (b + 1) * count)
-            zh[slot + b, 0:count, lanes], zl[slot + b, 0:count, lanes] = high[at], low[at]
-
-    def keep(slot, count, size, lanes, high, low, index):
-        for side, at in enumerate((slice(0, size), slice(count - size, count))):
-            high[index, side] = zh[slot, at, lanes]
-            low[index, side] = zl[slot, at, lanes]
-
-    for c in range(comps):
-        for sign, present in ((1, has_down), (-1, has_up)):
-            pl.when(present)(lambda sign=sign, c=c: copies[c, "v", sign].wait_recv())
+    def store(high, low, index, lanes, z):
+        high[index, 0:z.shape[0], lanes], low[index, 0:z.shape[0], lanes] = split(z)
+
+    def unpack(c):
         for g in range(groups):
             at = pl.ds(g * SUB, SUB)
             up, down = from_u[c, at, :], from_d[c, at, :]
             for q in range(per):
                 ext[c, pl.ds(g * width + q * SUB, SUB), cols:] = side_lanes(up, down, q, width)
-        store(c, rows, own, own_v[c] + y_halo(ext[c, :, cols:], margin, cols, gym))
-        store(c, rows, slice(cols, cols + LANES), y_ends(ext[c], margin, cols, gye))
-
-        def put(start, size, value, c=c):
-            coarse[c, pl.ds(start, size), :] = value
-
-        x_filter(zh.at[c], zl.at[c], 0, inner, everything, gxw, put)
-        keep(c, rows, width, everything, z1h, z1l, c)
-    store(0, inner, own, y_filter(stacked([coarse[c] for c in range(comps)]), margin, cols, tym))
+
+    def y_grid(c):
+        store(z1h, z1l, c, own, own_v[c] + y_halo(ext[c, :, cols:], margin, cols, gym))
+        store(z1h, z1l, c, slice(cols, cols + LANES), y_ends(ext[c], margin, cols, gye))
+
+    def x_grid(c):
+        def put(at, value):
+            coarse[c, at, :] = value
+
+        x_filter(z1h.at[c], z1l.at[c], inner, gxw, put)
+
+    def y_pair(p):
+        i, j = order[p]
+        store(zph, zpl, p, own, own_p[p] + y_halo(ext[i, :, cols:] * ext[j, :, cols:], margin, cols, gym))
+
+    def y_test(c):
+        store(z2h, z2l, c, own, y_filter(coarse[c], margin, cols, tym))
+
+    def x_test(c):
+        def put(at, value):
+            tested[c, at, :] = value
+
+        x_filter(z2h.at[c], z2l.at[c], innermost, txw, put)
+
+    def y_resolved(p):
+        i, j = order[p]
+        store(z2h, z2l, comps + p, own, y_filter(coarse[i] * coarse[j], margin, cols, tym))
+
+    def x_sub(p):
+        i, j = order[p]
+
+        def put(at, value):
+            sub[p, at, :] = value - coarse[i, at, own] * coarse[j, at, own]
+
+        x_filter(zph.at[p], zpl.at[p], inner, gxw, put)
+
+    def x_ger(p):
+        i, j = order[p]
+
+        def put(at, value):
+            ger[p, at, :] = value - tested[i, at, :] * tested[j, at, :]
+
+        x_filter(z2h.at[comps + p], z2l.at[comps + p], innermost, txw, put)
+
+    def arrive(c):
+        for sign, present in ((1, has_down), (-1, has_up)):
+            pl.when(present)(lambda sign=sign: copies[c, "v", sign].wait_recv())
+
     for c in range(comps):
-        def put_tested(start, size, value, c=c):
-            tested[c, pl.ds(start, size), :] = value
-
-        x_filter(zh.at[c], zl.at[c], 0, innermost, own, txw, put_tested)
-        keep(c, inner, width, own, z2h, z2l, c)
-
-    @pl.when(first)
-    def _():
-        pl.semaphore_wait(ready, 1 + vertical)
-        copies[-1, 0].start()
-        for sign, present in sides:
-            pl.when(present)(lambda sign=sign: copies[-1, sign].start())
-
-    @pl.loop(0, pairs // batch)
-    def _(step):
-        indices = [(step * batch + b,) + pair_of(step * batch + b) for b in range(batch)]
-        halos = y_halo(stacked([ext[i, :, cols:] * ext[j, :, cols:] for _, i, j in indices]), margin, cols, gym)
-        store(0, rows, own, stacked([own_p[p] for p, _, _ in indices]) + halos)
-        store(batch, inner, own,
-              y_filter(stacked([coarse[i] * coarse[j] for _, i, j in indices]), margin, cols, tym))
-        for b, (p, i, j) in enumerate(indices):
-            def put_sub(start, size, value, p=p, i=i, j=j):
-                at = pl.ds(start, size)
-                sub[p, at, :] = value - coarse[i, at, own] * coarse[j, at, own]
-
-            x_filter(zh.at[b], zl.at[b], 0, inner, own, gxw, put_sub)
-            keep(b, rows, width + margin, own, zph, zpl, p)
-        for b, (p, i, j) in enumerate(indices):
-            def put_ger(start, size, value, p=p, i=i, j=j):
-                at = pl.ds(start, size)
-                ger[p, at, :] = value - tested[i, at, :] * tested[j, at, :]
-
-            x_filter(zh.at[batch + b], zl.at[batch + b], 0, innermost, own, txw, put_ger)
-            keep(batch + b, inner, width, own, z2h, z2l, comps + p)
+        arrive(c)
+        unpack(c)
+        y_grid(c)
+        for p, (i, j) in enumerate(order):
+            if j == c:
+                y_pair(p)
+        if c > 0:
+            x_grid(c - 1)
+    column(first, lambda dy: forward(-1, dy))
+    x_grid(comps - 1)
+    for c in range(comps):
+        y_test(c)
+        x_sub(c)
+    for c in range(comps):
+        y_resolved(c)
+        x_test(c)
+
+    for p in range(comps, pairs):
+        y_resolved(p)
+        x_sub(p)
+        x_ger(p - comps)
+    for p in range(pairs - comps, pairs):
+        x_ger(p)
 
     copies[1, 0].wait_recv()
     copies[-1, 0].wait_recv()
@@ -392,9 +407,10 @@
         high, low = split(z)
         return [(high[n * size:(n + 1) * size], low[n * size:(n + 1) * size]) for n in range(count)]
 
-    def x_ends(side, late, high, low, weights):
-        h = (late[0], high) if side == 0 else (high, late[0])
-        l = (late[1], low) if side == 0 else (low, late[1])
+    def x_ends(side, late, high, low, n, count, size, weights):
+        at = slice(0, size) if side == 0 else slice(count - size, count)
+        h = (late[0], high[n, at]) if side == 0 else (high[n, at], late[0])
+        l = (late[1], low[n, at]) if side == 0 else (low[n, at], late[1])
         r = dot(weights, stacked(h + l))
         half = weights.shape[0] // 2
         return r[0:half] + r[half:]
@@ -410,12 +426,12 @@
     late = pieces(jnp.concatenate([z[0:count], y_ends(values, margin, cols, gye)], axis=1), width, len(both))
     coarse = {}
     for (c, side), part in zip(both, late):
-        coarse[c, side] = x_ends(side, part, z1h[c, side], z1l[c, side], gxe[...])
+        coarse[c, side] = x_ends(side, part, z1h, z1l, c, rows, width, gxe[...])
     late = pieces(z[count:], margin, len(every))
     for (p, side), part in zip(every, late):
         weights = stacked([gxe[0:margin], gxe[width:width + margin]] if side == 0 else
                           [gxe[width - margin:width], gxe[2 * width - margin:]])
-        value = x_ends(side, part, zph[p, side], zpl[p, side], weights)
+        value = x_ends(side, part, zph, zpl, p, rows, width + margin, weights)
         i, j = order[p]
         sub_e[p, side] = value - coarse[i, side][near[side], 0:cols] * coarse[j, side][near[side], 0:cols]
     leave(sub_e.at[:, 0], sub_ref.at[:, pl.ds(0, margin), :])
@@ -426,9 +442,9 @@
     late = pieces(z, width, len(both) + len(every))
     tested = {}
     for (c, side), part in zip(both, late):
-        tested[c, side] = x_ends(side, part, z2h[c, side], z2l[c, side], txe[...])
+        tested[c, side] = x_ends(side, part, z2h, z2l, c, inner, width, txe[...])
     for (p, side), part in zip(every, late[len(both):]):
-        value = x_ends(side, part, z2h[comps + p, side], z2l[comps + p, side], txe[...])
+        value = x_ends(side, part, z2h, z2l, comps + p, inner, width, txe[...])
         i, j = order[p]
         ger_e[p, side] = value - tested[i, side] * tested[j, side]
     leave(ger_e.at[:, 0], ger_ref.at[:, pl.ds(0, width), :])
@@ -445,29 +461,30 @@
     wide = cols + LANES
     step = LANES - width
     pairs = comps * (comps + 1) // 2
-    batch = 2
-    slots = max(comps, 2 * batch)
     vmem = pl.BlockSpec(memory_space=pltpu.VMEM)
     anywhere = pl.BlockSpec(memory_space=pl.ANY)
     packed = rows // width * SUB
     inner, innermost = rows - width, rows - 2 * width
-    filled = max((n + step - 1) // step * step + width for n in (inner, innermost))
+
+    def filled(count):
+        return round_up(count, step) + width
+
     fields = comps + pairs
     subs, gers = [], []
     shape = jax.ShapeDtypeStruct
     for plane in range(planes):
         v = jnp.swapaxes(velocity[:, plane], 1, 2)
         parts = pl.pallas_call(
-            functools.partial(interior_kernel, nx, ny, width, batch),
+            functools.partial(interior_kernel, nx, ny, width),
             out_shape=(
                 shape((2, comps, width, cols), F32),
                 shape((4, comps, SUB, LANES), F32),
-                shape((comps, 2, width, wide), BF),
-                shape((comps, 2, width, wide), BF),
-                shape((pairs, 2, width + margin, cols), BF),
-                shape((pairs, 2, width + margin, cols), BF),
-                shape((fields, 2, width, cols), BF),
-                shape((fields, 2, width, cols), BF),
+                shape((comps, max(rows, filled(inner)), wide), BF),
+                shape((comps, max(rows, filled(inner)), wide), BF),
+                shape((pairs, max(rows, filled(inner)), cols), BF),
+                shape((pairs, max(rows, filled(inner)), cols), BF),
+                shape((fields, max(inner, filled(innermost)), cols), BF),
+                shape((fields, max(inner, filled(innermost)), cols), BF),
                 shape((pairs, inner, cols), F32),
                 shape((pairs, innermost, cols), F32),
                 shape((2 * width, LANES), BF),
@@ -485,8 +502,8 @@
                 pltpu.VMEM((1, taps), F32),
                 pltpu.VMEM((taps, cols), F32),
                 pltpu.VMEM((round_up(taps, SUB), wide), F32),
-                pltpu.VMEM((2 * step, 2 * LANES), BF),
-                pltpu.VMEM((2 * step, 2 * LANES), BF),
+                pltpu.VMEM((step, 3 * LANES), BF),
+                pltpu.VMEM((step, 3 * LANES), BF),
                 pltpu.VMEM((comps, packed, LANES), F32),
                 pltpu.VMEM((comps, packed, LANES), F32),
                 pltpu.VMEM((comps, packed, LANES), F32),
@@ -497,15 +514,13 @@
                 pltpu.VMEM((pairs, rows, cols), F32),
                 pltpu.VMEM((comps, inner, wide), F32),
                 pltpu.VMEM((comps, innermost, cols), F32),
-                pltpu.VMEM((slots, max(rows, filled), wide), BF),
-                pltpu.VMEM((slots, max(rows, filled), wide), BF),
                 pltpu.SemaphoreType.DMA((5,)),
                 pltpu.SemaphoreType.DMA((8 + 2 * comps,)),
                 pltpu.SemaphoreType.DMA((8 + 2 * comps,)),
-                pltpu.SemaphoreType.REGULAR,
+                pltpu.SemaphoreType.REGULAR((7,)),
             ],
             compiler_params=pltpu.CompilerParams(
-                collective_id=plane, has_side_effects=True, vmem_limit_bytes=48 << 20),
+                collective_id=plane, has_side_effects=True, vmem_limit_bytes=20 << 20),
             name="interior",
         )(*[pltpu.with_memory_space_constraint(x, pltpu.HBM) for x in (
             v, grid_y.T, grid_x.reshape(1, taps), test_x.reshape(1, taps), test_y.T)])
@@ -520,7 +535,7 @@
                 pltpu.VMEM((pairs, 2, width, cols), F32),
                 pltpu.SemaphoreType.DMA((2 * pairs + 4,)),
             ],
-            compiler_params=pltpu.CompilerParams(vmem_limit_bytes=48 << 20),
+            compiler_params=pltpu.CompilerParams(vmem_limit_bytes=8 << 20),
             name="edge",
         )(*parts)
         subs.append(jnp.swapaxes(sub, 1, 2))

time: 17.6 us -> 16.6 us (0.943)
  Pallas kernels: 16.8 us -> 15.8 us
    pallas_call x1, Pallas kernels: 13.3 us -> 12.3 us  [local(): pl.pallas_call(functools.partial(interior_kernel, nx, ny, width), out_sha...]
where the time goes in v3:
time: 16.6 us; the launch traced here: 16.4 us
  Pallas kernels  15.8 us (95%)
  between operations  0.64 us (4%)
    pallas_call x1, Pallas kernels, local(): pl.pallas_call(functools.partial(interior_kernel, nx, ny, width), out_sha...  12.3 us
    pallas_call x1, Pallas kernels, local(): pl.pallas_call(functools.partial(edge_kernel, margin), out_shape=(out, ou...  3.49 us

profile of v3, /device:TPU:1, one launch (start us, length us, event | category | flops | bytes accessed | tf_op | source)
XLA Modules:
  0.0 16.4 jit_solution(18429646857832884304)
XLA Ops:
  0.6 12.3 %interior.1 = (f32[2,3,32,256]{3,2,1,0:T(8,128)S(1)}, f32[4,3,8,128]{3,2,1,0:T(8,128)S(1)}, bf16[3,320,384]{2,1,0:T(8,128)(2,1)S(1)}, bf16[3,320,384]{2,1,0:T(8,...) custom-call(f32[3,320,256]{2,1,0:T(8,128)} %bitcast.17, ...), custom_call_target="tpu_custom_call" | custom-call | tf_op jit(solution)/shard_map/interior/pallas_call | solution.py:477
  13.0 3.5 %edge.1 = (f32[6,320,256]{2,1,0:T(8,128)}, f32[6,320,256]{2,1,0:T(8,128)}) custom-call(f32[2,3,32,256]{3,2,1,0:T(8,128)S(1)} %get-tuple-element.19.halo, f32[4,3,8,128]{3,2,1,0:T(8,128)S(1)} %get-tuple-element.20.corners, bf16[3,320,384]{2,1,0:T(8,128)(2,1)S(1)} %get-tuple-element.21.z1h, bf16[3,320,384]{2,1,0:T(8,128)(2,1)S(1)} %get-tuple-element.22.z1l, ...), custom_call_target="tpu_custom_call" | custom-call | tf_op jit(solution)/shard_map/edge/pallas_call | solution.py:528

commit v4 on v3

--- a/solution.py
+++ b/solution.py
@@ -41,6 +41,13 @@
     high = high.astype(F32)
     edge[0:width] = (high + pltpu.roll(high, 2 * width, 1)).astype(BF)
     edge[width:] = low
+
+
+def spread(value, margin):
+    lane = lax.broadcasted_iota(jnp.int32, value.shape, 1)
+    near = jnp.where((lane < margin) | (lane >= LANES - margin), value, 0.0)
+    return pltpu.roll(jnp.where(lane < LANES // 2, near, 0.0), margin, 1) + pltpu.roll(
+        jnp.where(lane < LANES // 2, 0.0, near), LANES - margin, 1)
 
 
 def y_weights(table, taps, first_row, total, cols, main, edge=None, tiles=None):
@@ -68,14 +75,17 @@
             main[0:cols, at] = own_high
             main[cols:2 * cols, at] = own_low
             main[2 * cols:3 * cols, at] = own_high
+            halo = spread(halo, margin)
             high = halo.astype(BF).astype(F32)
-            packed = high + pltpu.roll(high, 2 * margin, 1) + pltpu.roll(halo - high, 4 * margin, 1)
+            packed = high + pltpu.roll(high, width, 1) + pltpu.roll(halo - high, 2 * width, 1)
             main[3 * cols:, at] = packed.T.astype(BF)
         else:
             low_own, high_own, halo = band[:, 0:LANES].T, band[:, cols - LANES:cols].T, band[:, cols:].T
             near = jnp.concatenate([
-                halo[0:width], low_own[0:LANES // 2 - width], high_own[LANES // 2 + width:],
-                halo[LANES - width:]], axis=0)
+                low_own[0:margin], halo[0:width], jnp.zeros((LANES - 2 * margin - 2 * width, LANES), F32),
+                halo[LANES - width:], high_own[LANES - margin:]], axis=0)
+            near = spread(near, margin)
+            near = near + pltpu.roll(near, width, 1) + pltpu.roll(near, 2 * width, 1)
             high, low = split(near)
             edge[0:LANES] = high
             edge[LANES:2 * LANES] = high
@@ -87,11 +97,22 @@
     return dot(jnp.concatenate([high, high, low], axis=1), main[0:3 * cols])
 
 
+def second(shape, width):
+    lane = lax.broadcasted_iota(jnp.int32, shape, 1)
+    return (lane < width // 2) | ((lane >= width + width // 2) & (lane < 2 * width))
+
+
+def thrice(halo, width):
+    lane = lax.broadcasted_iota(jnp.int32, halo.shape, 1)
+    margin = width // 2
+    home = ((lane >= margin) & (lane < width)) | ((lane >= LANES - width) & (lane < LANES - margin))
+    return jnp.where(home, halo, jnp.where(
+        second(halo.shape, width), pltpu.roll(halo, width, 1), pltpu.roll(halo, 2 * width, 1)))
+
+
 def packed_halo(halo, margin):
-    lane = lax.broadcasted_iota(jnp.int32, halo.shape, 1)
-    near = jnp.where((lane < margin) | (lane >= LANES - margin), halo, 0.0)
-    high = near.astype(BF).astype(F32)
-    return (high + pltpu.roll(near - high, 2 * margin, 1) + pltpu.roll(high, 4 * margin, 1)).astype(BF)
+    high = halo.astype(BF).astype(F32)
+    return jnp.where(second(halo.shape, 2 * margin), halo - high, high).astype(BF)
 
 
 def y_halo(halo, margin, cols, main):
@@ -103,21 +124,19 @@
     return dot(jnp.concatenate([high, high, low, packed_halo(value[:, cols:], margin)], axis=1), main[...])
 
 
-def y_ends(value, margin, cols, edge):
-    width = 2 * margin
-    halo = value[:, cols:]
+def y_ends(own, halo, margin, edge):
     lane = lax.broadcasted_iota(jnp.int32, halo.shape, 1)
-    own = jnp.where(lane < LANES // 2, pltpu.roll(value[:, 0:LANES], width, 1),
-                    pltpu.roll(value[:, cols - LANES:cols], LANES - width, 1))
-    high, low = split(jnp.where((lane < width) | (lane >= LANES - width), halo, own))
+    ends = jnp.where(lane < margin, own[:, 0:LANES],
+                     jnp.where(lane >= LANES - margin, own[:, own.shape[1] - LANES:], halo))
+    high, low = split(ends)
     return dot(jnp.concatenate([high, low, high], axis=1), edge[...])
 
 
 def side_lanes(up, down, q, width):
     lane = lax.broadcasted_iota(jnp.int32, up.shape, 1)
-    low = pltpu.roll(up, (LANES - q * width) % LANES, 1)
-    high = pltpu.roll(down, (LANES - (q + 1) * width) % LANES, 1)
-    return jnp.where(lane < width, low, jnp.where(lane >= LANES - width, high, 0.0))
+    margin = width // 2
+    return jnp.where(lane < LANES // 2, pltpu.roll(up, (LANES + margin - q * width) % LANES, 1),
+                     pltpu.roll(down, (2 * LANES - margin - (q + 1) * width) % LANES, 1))
 
 
 def x_filter(zh, zl, count, weights, put):
@@ -251,8 +270,15 @@
         pl.when(last & present)(lambda dy=dy: copies[1, dy].start())
         pl.when(not_first & present)(lambda dy=dy: copies[-1, dy].start())
 
+    def own_pair(p):
+        i, j = order[p]
+        own_p[p] = y_own(ext[i, :, own] * ext[j, :, own], cols, gym)
+
     for c in range(1, comps):
         own_v[c] = y_own(ext[c, :, own], cols, gym)
+    early = pairs // 2
+    for p in range(early):
+        own_pair(p)
 
     @pl.when(has_up)
     def _():
@@ -263,12 +289,14 @@
         pl.semaphore_wait(ready.at[(5 if dx > 0 else 1) + dy], 1)
         copies[dx, dy].start()
 
+    pl.when(not_last)(lambda: forward(1, 0))
     x_weights(gx_ref, gxw.shape[0], gxw, gxe)
     x_weights(tx_ref, txw.shape[0], txw, txe)
     y_weights(ty_ref[...], taps, first_row, total, cols, tym, tiles=own_tiles)
-    for p, (i, j) in enumerate(order):
-        own_p[p] = y_own(ext[i, :, own] * ext[j, :, own], cols, gym)
-    column(not_last, lambda dy: forward(1, dy))
+    for p in range(early, pairs):
+        own_pair(p)
+    for dy, present in sides:
+        pl.when(not_last & present)(lambda dy=dy: forward(1, dy))
 
     for sign, present, tile, at in ((1, has_down, t_low, LANES - margin), (-1, has_up, t_high, 0)):
         @pl.when(present)
@@ -281,16 +309,17 @@
     def store(high, low, index, lanes, z):
         high[index, 0:z.shape[0], lanes], low[index, 0:z.shape[0], lanes] = split(z)
 
-    def unpack(c):
+    def y_grid(c):
+        blocks = []
         for g in range(groups):
             at = pl.ds(g * SUB, SUB)
             up, down = from_u[c, at, :], from_d[c, at, :]
-            for q in range(per):
-                ext[c, pl.ds(g * width + q * SUB, SUB), cols:] = side_lanes(up, down, q, width)
-
-    def y_grid(c):
-        store(z1h, z1l, c, own, own_v[c] + y_halo(ext[c, :, cols:], margin, cols, gym))
-        store(z1h, z1l, c, slice(cols, cols + LANES), y_ends(ext[c], margin, cols, gye))
+            blocks += [side_lanes(up, down, q, width) for q in range(per)]
+        halo = stacked(blocks)
+        spread_halo = thrice(halo, width)
+        ext[c, :, cols:] = spread_halo
+        store(z1h, z1l, c, own, own_v[c] + y_halo(spread_halo, margin, cols, gym))
+        store(z1h, z1l, c, slice(cols, cols + LANES), y_ends(ext[c, :, own], halo, margin, gye))
 
     def x_grid(c):
         def put(at, value):
@@ -337,7 +366,6 @@
 
     for c in range(comps):
         arrive(c)
-        unpack(c)
         y_grid(c)
         for p, (i, j) in enumerate(order):
             if j == c:
@@ -400,8 +428,7 @@
 
     def ends(side, c):
         up, down = corners[2 + side, c], corners[side, c]
-        blocks = [side_lanes(up, down, q, width) for q in range(width // SUB)]
-        return jnp.concatenate([halo[side, c], jnp.concatenate(blocks, axis=0)], axis=1)
+        return halo[side, c], stacked([side_lanes(up, down, q, width) for q in range(width // SUB)])
 
     def pieces(z, size, count):
         high, low = split(z)
@@ -415,39 +442,53 @@
         half = weights.shape[0] // 2
         return r[0:half] + r[half:]
 
-    both = [(c, side) for c in range(comps) for side in range(2)]
-    every = [(p, side) for p in range(pairs) for side in range(2)]
     near = (slice(width - margin, width), slice(0, margin))
-    ext = {key: ends(key[1], key[0]) for key in both}
-    values = stacked([ext[key] for key in both])
-    products = stacked([ext[order[p][0], side][near[side]] * ext[order[p][1], side][near[side]] for p, side in every])
-    z = y_filter(stacked([values, products]), margin, cols, gym)
-    count = len(both) * width
-    late = pieces(jnp.concatenate([z[0:count], y_ends(values, margin, cols, gye)], axis=1), width, len(both))
-    coarse = {}
-    for (c, side), part in zip(both, late):
-        coarse[c, side] = x_ends(side, part, z1h, z1l, c, rows, width, gxe[...])
-    late = pieces(z[count:], margin, len(every))
-    for (p, side), part in zip(every, late):
+    everywhere = range(pairs)
+
+    def grid(side):
+        parts = [ends(side, c) for c in range(comps)]
+        rows_own, rows_halo = stacked([part[0] for part in parts]), stacked([part[1] for part in parts])
+        values = jnp.concatenate([rows_own, thrice(rows_halo, width)], axis=1)
+        ext = [values[c * width:(c + 1) * width] for c in range(comps)]
+        products = stacked([ext[i][near[side]] * ext[j][near[side]] for i, j in order])
+        z = y_filter(stacked([values, products]), margin, cols, gym)
+        count = comps * width
+        late = pieces(jnp.concatenate([z[0:count], y_ends(rows_own, rows_halo, margin, gye)], axis=1), width, comps)
+        return late, pieces(z[count:], margin, pairs)
+
+    def coarsen(side, late):
+        return [x_ends(side, part, z1h, z1l, c, rows, width, gxe[...]) for c, part in enumerate(late)]
+
+    def stress(side, coarse, late):
         weights = stacked([gxe[0:margin], gxe[width:width + margin]] if side == 0 else
                           [gxe[width - margin:width], gxe[2 * width - margin:]])
-        value = x_ends(side, part, zph, zpl, p, rows, width + margin, weights)
-        i, j = order[p]
-        sub_e[p, side] = value - coarse[i, side][near[side], 0:cols] * coarse[j, side][near[side], 0:cols]
+        for p, part in enumerate(late):
+            value = x_ends(side, part, zph, zpl, p, rows, width + margin, weights)
+            i, j = order[p]
+            sub_e[p, side] = value - coarse[i][near[side], 0:cols] * coarse[j][near[side], 0:cols]
+
+    def test(side, coarse):
+        z = y_filter(stacked(coarse + [coarse[i] * coarse[j] for i, j in order]), margin, cols, tym)
+        return pieces(z, width, comps + pairs)
+
+    def resolve(side, late):
+        tested = [x_ends(side, part, z2h, z2l, c, inner, width, txe[...]) for c, part in enumerate(late[0:comps])]
+        for p, part in enumerate(late[comps:]):
+            i, j = order[p]
+            ger_e[p, side] = (x_ends(side, part, z2h, z2l, comps + p, inner, width, txe[...])
+                              - tested[i] * tested[j])
+
+    late = [grid(side) for side in range(2)]
+    coarse = [coarsen(side, late[side][0]) for side in range(2)]
+    tests = []
+    for side in range(2):
+        tests.append(test(side, coarse[side]))
+        stress(side, coarse[side], late[side][1])
     leave(sub_e.at[:, 0], sub_ref.at[:, pl.ds(0, margin), :])
     leave(sub_e.at[:, 1], sub_ref.at[:, pl.ds(rows - margin, margin), :])
-    z = y_filter(stacked([coarse[key] for key in both]
-                         + [coarse[order[p][0], side] * coarse[order[p][1], side] for p, side in every]),
-                 margin, cols, tym)
-    late = pieces(z, width, len(both) + len(every))
-    tested = {}
-    for (c, side), part in zip(both, late):
-        tested[c, side] = x_ends(side, part, z2h, z2l, c, inner, width, txe[...])
-    for (p, side), part in zip(every, late[len(both):]):
-        value = x_ends(side, part, z2h, z2l, comps + p, inner, width, txe[...])
-        i, j = order[p]
-        ger_e[p, side] = value - tested[i, side] * tested[j, side]
+    resolve(0, tests[0])
     leave(ger_e.at[:, 0], ger_ref.at[:, pl.ds(0, width), :])
+    resolve(1, tests[1])
     leave(ger_e.at[:, 1], ger_ref.at[:, pl.ds(rows - width, width), :])
     for copy in outs:
         copy.wait()

time: 16.6 us -> 16.2 us (0.976)
  Pallas kernels: 15.8 us -> 15.4 us
    pallas_call x1, Pallas kernels: 3.49 us -> 3.08 us  [local(): pl.pallas_call(functools.partial(edge_kernel, margin), out_shape=(out, ou...]
where the time goes in v4:
time: 16.2 us; the launch traced here: 16.1 us
  Pallas kernels  15.4 us (95%)
  between operations  0.64 us (4%)
    pallas_call x1, Pallas kernels, local(): pl.pallas_call(functools.partial(interior_kernel, nx, ny, width), out_sha...  12.3 us
    pallas_call x1, Pallas kernels, local(): pl.pallas_call(functools.partial(edge_kernel, margin), out_shape=(out, ou...  3.08 us

profile of v4, /device:TPU:1, one launch (start us, length us, event | category | flops | bytes accessed | tf_op | source)
XLA Modules:
  0.0 16.1 jit_solution(3463784085618228721)
XLA Ops:
  0.6 12.3 %interior.1 = (f32[2,3,32,256]{3,2,1,0:T(8,128)S(1)}, f32[4,3,8,128]{3,2,1,0:T(8,128)S(1)}, bf16[3,320,384]{2,1,0:T(8,128)(2,1)S(1)}, bf16[3,320,384]{2,1,0:T(8,...) custom-call(f32[3,320,256]{2,1,0:T(8,128)} %bitcast.17, ...), custom_call_target="tpu_custom_call" | custom-call | tf_op jit(solution)/shard_map/interior/pallas_call | solution.py:518
  13.0 3.1 %edge.1 = (f32[6,320,256]{2,1,0:T(8,128)}, f32[6,320,256]{2,1,0:T(8,128)}) custom-call(f32[2,3,32,256]{3,2,1,0:T(8,128)S(1)} %get-tuple-element.19.halo, f32[4,3,8,128]{3,2,1,0:T(8,128)S(1)} %get-tuple-element.20.corners, bf16[3,320,384]{2,1,0:T(8,128)(2,1)S(1)} %get-tuple-element.21.z1h, bf16[3,320,384]{2,1,0:T(8,128)(2,1)S(1)} %get-tuple-element.22.z1l, ...), custom_call_target="tpu_custom_call" | custom-call | tf_op jit(solution)/shard_map/edge/pallas_call | solution.py:569

commit v5 on v4

--- a/solution.py
+++ b/solution.py
@@ -188,8 +188,7 @@
     own = slice(0, cols)
     order = [(i, j) for i in range(comps) for j in range(i, comps)]
     loads = [pltpu.make_async_copy(src, dst, load_sem.at[i]) for i, (src, dst) in enumerate((
-        (t_hbm, t_ref), (gx_hbm, gx_ref), (tx_hbm, tx_ref), (ty_hbm, ty_ref),
-        (v_hbm, ext.at[:, :, own])))]
+        (v_hbm, ext.at[:, :, own]), (t_hbm, t_ref), (gx_hbm, gx_ref), (tx_hbm, tx_ref), (ty_hbm, ty_ref)))]
     for load in loads:
         load.start()
 
@@ -224,6 +223,23 @@
 
     column(last, lambda dy: signal(ready.at[1 - dy], 1, dy))
 
+    @pl.when(not_last & (not_first | has_down))
+    def _():
+        pl.semaphore_wait(barrier, jnp.where(has_down, 1, 0) + jnp.where(first, 0, 1 + vertical))
+
+    pl.when(not_first)(lambda: copies[-1, 0].start())
+    pl.when(has_down)(lambda: signal(ready.at[3], 0, -1))
+    column(not_first, lambda dy: signal(ready.at[5 - dy], -1, dy))
+
+    loads[0].wait()
+    for c in range(comps):
+        for g in range(groups):
+            for q in range(per):
+                src = pl.ds(g * width + q * SUB, SUB)
+                dst = pl.ds(g * SUB, SUB)
+                pack_u[c, dst, q * width:(q + 1) * width] = ext[c, src, cols - width:cols]
+                pack_d[c, dst, q * width:(q + 1) * width] = ext[c, src, 0:width]
+
     text_ref[...] = jnp.zeros_like(text_ref)
     for z, full in ((z1h, rows), (z1l, rows), (zph, rows), (zpl, rows), (z2h, inner), (z2l, inner)):
         if z.shape[1] > full:
@@ -235,65 +251,46 @@
             for side in range(2):
                 corners[side + (2 if sign > 0 else 0)] = jnp.zeros(corners.shape[1:], F32)
 
-    for load in loads[:4]:
+    def wall(sign):
+        copies["t", sign].start()
+        for c in range(comps):
+            copies[c, "v", sign].start()
+
+    loads[1].wait()
+    pl.when(has_down)(lambda: wall(-1))
+    @pl.when(has_up)
+    def _():
+        pl.semaphore_wait(ready.at[3], 1)
+        wall(1)
+
+    for dy, present in sides:
+        pl.when(last & present)(lambda dy=dy: copies[1, dy].start())
+        pl.when(not_first & present)(lambda dy=dy: copies[-1, dy].start())
+
+    for load in loads[2:]:
         load.wait()
     text_ref[0:taps, 0:cols] = t_ref[...]
     first_row, total = me_y * cols, cols * ny
     own_tiles = range(cols // LANES)
     y_weights(t_ref[...], taps, first_row, total, cols, gym, tiles=own_tiles)
 
-    @pl.when(not_last & (not_first | has_down))
-    def _():
-        pl.semaphore_wait(barrier, jnp.where(has_down, 1, 0) + jnp.where(first, 0, 1 + vertical))
-
-    pl.when(not_first)(lambda: copies[-1, 0].start())
-    pl.when(has_down)(lambda: signal(ready.at[3], 0, -1))
-    column(not_first, lambda dy: signal(ready.at[5 - dy], -1, dy))
-
-    loads[4].wait()
-    for c in range(comps):
-        for g in range(groups):
-            for q in range(per):
-                src = pl.ds(g * width + q * SUB, SUB)
-                dst = pl.ds(g * SUB, SUB)
-                pack_u[c, dst, q * width:(q + 1) * width] = ext[c, src, cols - width:cols]
-                pack_d[c, dst, q * width:(q + 1) * width] = ext[c, src, 0:width]
-
-    def wall(sign):
-        copies["t", sign].start()
-        for c in range(comps):
-            copies[c, "v", sign].start()
-
-    own_v[0] = y_own(ext[0, :, own], cols, gym)
-    pl.when(has_down)(lambda: wall(-1))
-    for dy, present in sides:
-        pl.when(last & present)(lambda dy=dy: copies[1, dy].start())
-        pl.when(not_first & present)(lambda dy=dy: copies[-1, dy].start())
-
     def own_pair(p):
         i, j = order[p]
         own_p[p] = y_own(ext[i, :, own] * ext[j, :, own], cols, gym)
 
-    for c in range(1, comps):
-        own_v[c] = y_own(ext[c, :, own], cols, gym)
-    early = pairs // 2
-    for p in range(early):
-        own_pair(p)
-
-    @pl.when(has_up)
-    def _():
-        pl.semaphore_wait(ready.at[3], 1)
-        wall(1)
-
     def forward(dx, dy):
         pl.semaphore_wait(ready.at[(5 if dx > 0 else 1) + dy], 1)
         copies[dx, dy].start()
 
+    for c in range(comps):
+        own_v[c] = y_own(ext[c, :, own], cols, gym)
+    for p in range(0):
+        own_pair(p)
     pl.when(not_last)(lambda: forward(1, 0))
     x_weights(gx_ref, gxw.shape[0], gxw, gxe)
     x_weights(tx_ref, txw.shape[0], txw, txe)
     y_weights(ty_ref[...], taps, first_row, total, cols, tym, tiles=own_tiles)
-    for p in range(early, pairs):
+    for p in range(0, pairs):
         own_pair(p)
     for dy, present in sides:
         pl.when(not_last & present)(lambda dy=dy: forward(1, dy))

time: 16.2 us -> 15.7 us (0.969)
  Pallas kernels: 15.4 us -> 14.9 us
    pallas_call x1, Pallas kernels: 12.3 us -> 11.8 us  [local(): pl.pallas_call(functools.partial(interior_kernel, nx, ny, width), out_sha...]
where the time goes in v5:
time: 15.7 us; the launch traced here: 15.5 us
  Pallas kernels  14.9 us (95%)
  between operations  0.64 us (4%)
    pallas_call x1, Pallas kernels, local(): pl.pallas_call(functools.partial(interior_kernel, nx, ny, width), out_sha...  11.8 us
    pallas_call x1, Pallas kernels, local(): pl.pallas_call(functools.partial(edge_kernel, margin), out_shape=(out, ou...  3.08 us

profile of v5, /device:TPU:1, one launch (start us, length us, event | category | flops | bytes accessed | tf_op | source)
XLA Modules:
  0.0 15.5 jit_solution(9973497142533403670)
XLA Ops:
  0.6 11.8 %interior.1 = (f32[2,3,32,256]{3,2,1,0:T(8,128)S(1)}, f32[4,3,8,128]{3,2,1,0:T(8,128)S(1)}, bf16[3,320,384]{2,1,0:T(8,128)(2,1)S(1)}, bf16[3,320,384]{2,1,0:T(8,...) custom-call(f32[3,320,256]{2,1,0:T(8,128)} %bitcast.17, ...), custom_call_target="tpu_custom_call" | custom-call | tf_op jit(solution)/shard_map/interior/pallas_call | solution.py:515
  12.4 3.1 %edge.1 = (f32[6,320,256]{2,1,0:T(8,128)}, f32[6,320,256]{2,1,0:T(8,128)}) custom-call(f32[2,3,32,256]{3,2,1,0:T(8,128)S(1)} %get-tuple-element.19.halo, f32[4,3,8,128]{3,2,1,0:T(8,128)S(1)} %get-tuple-element.20.corners, bf16[3,320,384]{2,1,0:T(8,128)(2,1)S(1)} %get-tuple-element.21.z1h, bf16[3,320,384]{2,1,0:T(8,128)(2,1)S(1)} %get-tuple-element.22.z1l, ...), custom_call_target="tpu_custom_call" | custom-call | tf_op jit(solution)/shard_map/edge/pallas_call | solution.py:566
